TPU v7x, 256 devices: a whole 4x4x8 slice. The times are simulated.
256 devices in a mesh: fx: 32 (over z, y), fy: 4 (over x), fz: 2 (over core).
Axes of the slice: x: 4, y: 4, z: 8, core: 2. Of those that a mesh axis runs over, the one named last changes fastest.
Arguments:
- state: float32 [5, 16, 1024, 512], P(None, 'fz', 'fx', 'fy'), may hold values from -6 to 6
- kappa: float32 [16, 1024, 512], P('fz', 'fx', 'fy'), may hold values from 0.25 to 1
- mix: float32 [5, 5], replicated, may hold values from -0.16 to 0.16
- press_weight: float32 [5], replicated, may hold values from 0.5 to 1.5
- source_weight: float32 [5], replicated, may hold values from 0.05 to 0.2
- interp: float32 [128, 128], replicated, may hold values from -0.25 to 0.25
- block_inverse: float32 [512, 128, 128], P('fx'), as said below
- coupling: float32 [512, 128, 128], P('fx'), may hold values from -0.125 to 0.125
- front_order: int32 [32, 16], P('fx'), may hold values from 0 to 15, each once within a row
- face_owner: int32 [4096, 1], P(('fx', 'fy')), may hold values from 0 to 31; in each aligned block of 32 rows (0 to 31, 32 to 63, ...) at most 2 rows name the same one
- face_slot: int32 [4096], P(('fx', 'fy')), may hold values from 0 to 15
Outputs:
- state_out: float32 [5, 16, 1024, 512], P(None, 'fz', 'fx', 'fy')
- displacement: float32 [512, 128], P('fx')
Inputs may be any that keep to these rules, and one draw needn't show every extreme that they name: `face_owner`: in the rows of one device no owner is named more than 2 times; every draw has some device naming one owner exactly 2 times. `front_order`: each row lists every block of one owner once. `block_inverse`: each block is the inverse of a stiffness block.
All inputs are finite; a program needn't handle non-finite values.
Results may differ from a plain program's by a relative error of at most 0.00021.
Values sent between devices are 32-bit elements; how exact they have to be, the bound alone decides.
A program may use at most 64 MiB of HBM per device.

v0:
```python
import jax
import jax.numpy as jnp
from jax import lax
from jax.sharding import PartitionSpec as P

ITERS = 3


DIFFUSION = 0.16
HIGHEST = lax.Precision.HIGHEST


def with_halo(cells, sides, width):
    for axis, dim in sides:
        count = lax.axis_size(axis)
        ends = count - 1
        head = lax.slice_in_dim(cells, 0, width, axis=dim)
        tail = lax.slice_in_dim(cells, cells.shape[dim] - width, cells.shape[dim], axis=dim)
        cells = jnp.concatenate(
            [
                lax.ppermute(tail, axis, [(i, (i + 1) % count) for i in range(ends)]),
                cells,
                lax.ppermute(head, axis, [((i + 1) % count, i) for i in range(ends)]),
            ],
            axis=dim,
        )
    return cells


def sweep_core(padded, coeff, mix):
    centre = padded[:, 1:-1, 1:-1, 1:-1]
    beside = padded[:, 2:, 1:-1, 1:-1] + padded[:, :-2, 1:-1, 1:-1]
    beside = beside + padded[:, 1:-1, 2:, 1:-1] + padded[:, 1:-1, :-2, 1:-1]
    beside = beside + padded[:, 1:-1, 1:-1, 2:] + padded[:, 1:-1, 1:-1, :-2]
    mixed = jnp.einsum("cd,dzxy->czxy", mix, centre, precision=HIGHEST)
    return centre + DIFFUSION * coeff[None] * (beside - 6.0 * centre) + mixed


def frontal(block_loads, inverse, coupling, order):
    blocks_owner, block_dofs = block_loads.shape

    def advance(position, carry):
        previous, solved = carry
        target = order[position]
        right_side = block_loads[target] - jnp.dot(coupling[target], previous, precision=HIGHEST)
        current = jnp.dot(inverse[target], right_side, precision=HIGHEST)
        return (current, solved.at[target].set(current))

    start = (
        jnp.zeros((block_dofs,), jnp.float32),
        jnp.zeros((blocks_owner, block_dofs), jnp.float32),
    )
    return lax.fori_loop(0, blocks_owner, advance, start)[1]


def on_device(
    state,
    kappa,
    mix,
    press_weight,
    source_weight,
    interp,
    block_inverse,
    coupling,
    front_order,
    face_owner,
    face_slot,
):
    count_z, count_x, count_y = kappa.shape
    blocks_owner = block_inverse.shape[0]
    owners = lax.axis_size("fx")
    wall_mask = (lax.axis_index("fz") == 0).astype(jnp.float32)
    total_z = count_z * lax.axis_size("fz")
    heights = (lax.axis_index("fz") * count_z + jnp.arange(count_z)).astype(jnp.float32)
    profile = 1.0 - heights / total_z
    owner_of = face_owner[:, 0]
    spread = (
        jnp.arange(owners * blocks_owner)[:, None] == (owner_of * blocks_owner + face_slot)[None, :]
    ).astype(jnp.float32)
    displacement = jnp.zeros((blocks_owner, interp.shape[1]), jnp.float32)
    for iteration in range(ITERS):
        for sweep_index in range(2):
            padded = with_halo(state, (("fx", 2), ("fy", 3), ("fz", 1)), 1)
            state = sweep_core(padded, kappa, mix)
        pressure = jnp.sum(press_weight[:, None, None] * state[:, 0], axis=0) * wall_mask
        outgoing = jnp.dot(spread, pressure, precision=HIGHEST)
        incoming = lax.all_to_all(outgoing, "fx", split_axis=0, concat_axis=0, tiled=True)
        forces = jnp.sum(incoming.reshape(owners, blocks_owner, count_y), axis=0)
        forces = lax.psum(forces, ("fy", "fz"))
        block_loads = jnp.dot(forces, interp, precision=HIGHEST)
        displacement = frontal(block_loads, block_inverse, coupling, front_order[0])
        face_disp = jnp.dot(displacement, interp.T, precision=HIGHEST)
        every_block = lax.all_gather(face_disp, "fx", axis=0, tiled=True)
        wall_disp = jnp.dot(spread.T, every_block, precision=HIGHEST)
        state = (
            state
            + source_weight[:, None, None, None]
            * profile[None, :, None, None]
            * wall_disp[None, None]
        )
    return (state, displacement)


def solution(mesh):
    return jax.shard_map(
        on_device,
        mesh=mesh,
        in_specs=(
            P(None, "fz", "fx", "fy"),
            P("fz", "fx", "fy"),
            P(),
            P(),
            P(),
            P(),
            P("fx", None, None),
            P("fx", None, None),
            P("fx", None),
            P(("fx", "fy"), None),
            P(("fx", "fy")),
        ),
        out_specs=(P(None, "fz", "fx", "fy"), P("fx", None)),
        check_vma=False,
    )
```

profile of v0, /device:TPU:8, one launch (start us, length us, event | category | flops | bytes accessed | tf_op | source)
XLA Modules:
  0.0 744.5 jit_solution(12291830759761344540)
XLA Ops:
  20.3 3.8 collective-permute-done.3
  40.5 4.8 collective-permute-done.7
  52.5 3.9 collective-permute-done.9
  60.0 4.5 collective-permute-start.11
  65.3 4.5 fusion.37
  71.9 13.9 %all-to-all-start = ((f32[32,16,128]{2,1,0:T(8,128)}), f32[32,16,128]{2,1,0:T(8,128)S(1)}, u32[]{:S(2)}, u32[]{:S(2)}) async-start(f32[32,16,128]{2,1,0:T(8,128)} %bitcast.34), calls=%async_computation | async-start | bytes 524288 | tf_op jit(solution)/shard_map/all_to_all | solution.py:87
  86.6 10.9 %all-to-all-done = f32[32,16,128]{2,1,0:T(8,128)S(1)} async-done(((f32[32,16,128]{2,1,0:T(8,128)}), f32[32,16,128]{2,1,0:T(8,128)S(1)}, u32[]{:S(2)}, u32[]{:S(2)}) %all-to-all-start) | async-done | bytes 262176 | tf_op jit(solution)/shard_map/all_to_all | solution.py:87
  97.5 12.7 %psum.21 = f32[16,128]{1,0:T(8,128)S(1)} all-reduce(f32[16,128]{1,0:T(8,128)S(1)} %reduce_sum.55), channel_id=1, replica_groups=mesh['fx'=32,'fy'=4,'fz'=2] {'fy','fz'}, use_global_device_ids=true, to_apply=%region_2.0 | all-reduce | flops 2048 | bytes 16384 | tf_op jit(solution)/shard_map/psum | solution.py:89
  110.4 97.6 %while.48 = (s32[]{:T(128)}, f32[128]{0:T(128)S(1)}, f32[16,128]{1,0:T(8,128)S(1)}, s32[16]{0:T(128)S(1)}, f32[16,128,128]{2,1,0:T(8,128)}, /*index=5*/f32[16,12...) while((s32[]{:T(128)}, f32[128]{0:T(128)S(1)}, ...), condition=%wide.region_5.0_spmd, body=%wide.region_3.0_spmd.sunk | while | flops 393486 | bytes 138424 | solution.py:53
  208.2 48.1 %all_gather.9 = f32[512,128]{1,0:T(8,128)S(1)} all-gather(f32[16,128]{1,0:T(8,128)S(1)} %fusion.129), channel_id=1, replica_groups=mesh['fx'=32,'fy'=4,'fz'=2] {'fx'}, dimensions={0}, use_global_device_ids=true | all-gather | bytes 270336 | tf_op jit(solution)/shard_map/all_gather | solution.py:93
  284.5 3.9 collective-permute-start.18
  290.4 5.4 collective-permute-done.19
  319.3 10.7 %all-to-all-start.1 = ((f32[32,16,128]{2,1,0:T(8,128)}), f32[32,16,128]{2,1,0:T(8,128)S(1)}, u32[]{:S(2)}, u32[]{:S(2)}) async-start(f32[32,16,128]{2,1,0:T(8,128)} %bitcast.38), calls=%async_computation.1 | async-start | bytes 524288 | tf_op jit(solution)/shard_map/all_to_all | solution.py:87
  329.9 11.7 %all-to-all-done.1 = f32[32,16,128]{2,1,0:T(8,128)S(1)} async-done(((f32[32,16,128]{2,1,0:T(8,128)}), f32[32,16,128]{2,1,0:T(8,128)S(1)}, u32[]{:S(2)}, u32[]{:S(2)}) %all-to-all-start.1) | async-done | bytes 262176 | tf_op jit(solution)/shard_map/all_to_all | solution.py:87
  341.7 12.7 %psum.22 = f32[16,128]{1,0:T(8,128)S(1)} all-reduce(f32[16,128]{1,0:T(8,128)S(1)} %reduce_sum.57), channel_id=1, replica_groups=mesh['fx'=32,'fy'=4,'fz'=2] {'fy','fz'}, use_global_device_ids=true, to_apply=%region_8.0 | all-reduce | flops 2048 | bytes 16384 | tf_op jit(solution)/shard_map/psum | solution.py:89
  354.6 97.6 %while.49 = (s32[]{:T(128)}, f32[128]{0:T(128)S(1)}, f32[16,128]{1,0:T(8,128)S(1)}, s32[16]{0:T(128)S(1)}, f32[16,128,128]{2,1,0:T(8,128)}, /*index=5*/f32[16,12...) while((s32[]{:T(128)}, f32[128]{0:T(128)S(1)}, ...), condition=%wide.region_11.0_spmd, body=%wide.region_9.0_spmd.sunk | while | flops 393486 | bytes 138424 | solution.py:53
  452.3 48.1 %all_gather.10 = f32[512,128]{1,0:T(8,128)S(1)} all-gather(f32[16,128]{1,0:T(8,128)S(1)} %fusion.131), channel_id=1, replica_groups=mesh['fx'=32,'fy'=4,'fz'=2] {'fx'}, dimensions={0}, use_global_device_ids=true | all-gather | bytes 270336 | tf_op jit(solution)/shard_map/all_gather | solution.py:93
  528.7 3.9 collective-permute-start.30
  534.6 5.4 collective-permute-done.31
  562.4 10.8 %all-to-all-start.2 = ((f32[32,16,128]{2,1,0:T(8,128)}), f32[32,16,128]{2,1,0:T(8,128)S(1)}, u32[]{:S(2)}, u32[]{:S(2)}) async-start(f32[32,16,128]{2,1,0:T(8,128)} %bitcast.42), calls=%async_computation.2 | async-start | bytes 524288 | tf_op jit(solution)/shard_map/all_to_all | solution.py:87
  573.2 11.7 %all-to-all-done.2 = f32[32,16,128]{2,1,0:T(8,128)S(1)} async-done(((f32[32,16,128]{2,1,0:T(8,128)}), f32[32,16,128]{2,1,0:T(8,128)S(1)}, u32[]{:S(2)}, u32[]{:S(2)}) %all-to-all-start.2) | async-done | bytes 262176 | tf_op jit(solution)/shard_map/all_to_all | solution.py:87
  585.0 12.7 %psum.23 = f32[16,128]{1,0:T(8,128)S(1)} all-reduce(f32[16,128]{1,0:T(8,128)S(1)} %reduce_sum.59), channel_id=1, replica_groups=mesh['fx'=32,'fy'=4,'fz'=2] {'fy','fz'}, use_global_device_ids=true, to_apply=%region_14.0 | all-reduce | flops 2048 | bytes 16384 | tf_op jit(solution)/shard_map/psum | solution.py:89
  597.9 97.0 %while.50 = (s32[]{:T(128)}, f32[128]{0:T(128)S(1)}, f32[16,128]{1,0:T(8,128)S(1)}, s32[16]{0:T(128)S(1)}, f32[16,128,128]{2,1,0:T(8,128)}, /*index=5*/f32[16,12...) while((s32[]{:T(128)}, f32[128]{0:T(128)S(1)}, ...), condition=%wide.region_17.0_spmd, body=%wide.region_15.0_spmd.sunk | while | flops 393486 | bytes 138424 | solution.py:53
  695.1 47.9 %all_gather.11 = f32[512,128]{1,0:T(8,128)S(1)} all-gather(f32[16,128]{1,0:T(8,128)S(1)} %fusion.133), channel_id=1, replica_groups=mesh['fx'=32,'fy'=4,'fz'=2] {'fx'}, dimensions={0}, use_global_device_ids=true | all-gather | bytes 270336 | tf_op jit(solution)/shard_map/all_gather | solution.py:93
  (448 shorter events, 356.5 us)
Async XLA Ops:
  2.2 5.9 collective-permute-start
  5.7 5.8 collective-permute-start.1
  14.6 5.1 collective-permute-start.2
  18.4 5.7 collective-permute-start.3
  34.6 5.9 collective-permute-start.6
  37.8 7.5 %collective-permute-start.7 = (f32[5,8,1,128]{3,0,2,1:T(8,128)S(1)}, f32[5,8,1,128]{3,0,2,1:T(8,128)S(1)}, u32[]{:S(2)}, u32[]{:S(2)}) collective-permute-start(f32[5,8,1,128]{3,0,2,1:T(8,128)S(1)} %get-tuple-element.528), channel_id=1, source_target_pairs={{8,0},{16,8},{24,16},{32,24},{40,32},{48,40},{56,48},{64,56},{72,6... | collective-permute-start | bytes 61448 | tf_op jit(solution)/shard_map/ppermute | solution.py:23
  50.6 5.8 collective-permute-start.9
  58.8 5.8 collective-permute-start.10
  60.0 5.2 collective-permute-start.11
  71.9 25.6 %all-to-all-start = ((f32[32,16,128]{2,1,0:T(8,128)}), f32[32,16,128]{2,1,0:T(8,128)S(1)}, u32[]{:S(2)}, u32[]{:S(2)}) async-start(f32[32,16,128]{2,1,0:T(8,128)} %bitcast.34), calls=%async_computation | async-start | bytes 524288 | tf_op jit(solution)/shard_map/all_to_all | solution.py:87
  256.8 5.9 collective-permute-start.12
  259.3 5.8 collective-permute-start.13
  268.4 5.7 collective-permute-start.15
  284.5 5.9 collective-permute-start.18
  288.5 7.4 collective-permute-start.19
  301.0 5.7 collective-permute-start.21
  319.3 22.4 %all-to-all-start.1 = ((f32[32,16,128]{2,1,0:T(8,128)}), f32[32,16,128]{2,1,0:T(8,128)S(1)}, u32[]{:S(2)}, u32[]{:S(2)}) async-start(f32[32,16,128]{2,1,0:T(8,128)} %bitcast.38), calls=%async_computation.1 | async-start | bytes 524288 | tf_op jit(solution)/shard_map/all_to_all | solution.py:87
  501.0 5.9 collective-permute-start.24
  503.5 5.8 collective-permute-start.25
  512.6 5.7 collective-permute-start.27
  528.7 5.9 collective-permute-start.30
  532.7 7.4 collective-permute-start.31
  545.2 5.7 collective-permute-start.33
  562.4 22.5 %all-to-all-start.2 = ((f32[32,16,128]{2,1,0:T(8,128)}), f32[32,16,128]{2,1,0:T(8,128)S(1)}, u32[]{:S(2)}, u32[]{:S(2)}) async-start(f32[32,16,128]{2,1,0:T(8,128)} %bitcast.42), calls=%async_computation.2 | async-start | bytes 524288 | tf_op jit(solution)/shard_map/all_to_all | solution.py:87
  (43 other events, 881.7 us)
where the time goes:
time: 752 us; the launch traced here: 744 us
  blocking collectives  182 us (24%)
  matrix products  149 us (20%)
  starting transfers between devices  118 us (16%)
  loops' own time  94.4 us (13%)
  waiting for transfers between devices  87.3 us (12%)
  local copies, waits for them, and re-layouts  64.7 us (9%)
  other arithmetic  46.7 us (6%)
    all_gather x3, blocking collectives, on_device(): every_block = lax.all_gather(face_disp, 'fx', axis=0, tiled=True)  144 us
    another operation x3, loops' own time, frontal(): return lax.fori_loop(0, blocks_owner, advance, start)[1]  94.4 us
    dot_general x48, matrix products, advance(): current = jnp.dot(inverse[target], right_side, precision=HIGHEST)  81.6 us
    ppermute x18, starting transfers between devices, with_halo(): lax.ppermute(tail, axis, [(i, (i + 1) % count) for i in range(ends)])  51.9 us
    dot_general x48, matrix products, advance(): jnp.dot(coupling[target], previous, precision=HIGHEST)  48.8 us
    ppermute x18, waiting for transfers between devices, with_halo(): lax.ppermute(head, axis, [((i + 1) % count, i) for i in range(ends)])  46.5 us
    psum x3, blocking collectives, on_device(): forces = lax.psum(forces, ('fy', 'fz'))  38 us
    another operation x48, other arithmetic  36.6 us
  transfers between devices with their start and end apart: 39, of which 21 were waited for; matrix products, arithmetic and copies ran while one was open for 1% of the time, Pallas kernels for 0%

commit v1 on v0

v1 whole, which is shorter than its diff:
```python
import functools

import jax
import jax.numpy as jnp
from jax import lax
from jax.experimental import pallas as pl
from jax.experimental.pallas import tpu as pltpu
from jax.sharding import PartitionSpec as P

ITERS = 3
DIFFUSION = 0.16
HIGHEST = lax.Precision.HIGHEST
MESH = pl.DeviceIdType.MESH
F32 = jnp.float32
BF16 = jnp.bfloat16

NV, NZL, CX, CY = 5, 8, 32, 128
NFX, NFY = 32, 4
RING_Z, RING_Y = 8, 4
EB, EBD, CAP = 128, 16, 2
FACES = NFX * NFY * CAP
NT = (((1,), (1,)), ((), ()))


def far_first(step, ring):
    return ring // 2 + (1 - 2 * (step % 2)) * ((step + 1) // 2)


def split(values):
    high = values.astype(BF16)
    return high, (values - high.astype(F32)).astype(BF16)


def pick(selector, values):
    high, low = split(values)
    return jnp.dot(selector, high, preferred_element_type=F32) + jnp.dot(selector, low, preferred_element_type=F32)


def kernel(
    state_in, kappa_in, mix, press_weight, source_weight, interp, inverse_in, coupling_in, order, owner, slot,
    state_out, disp_out,
    S, K, BI, CO, R, XS, XR, YS, YR, ZR, SF, RF, SD, RD, FP, FPT, AM, AT, FR, XV, DV, DR,
    load_sem, hsend, hrecv, fsend, frecv, dsend, drecv, osend, orecv,
):
    ix, iy, iz = lax.axis_index("fx"), lax.axis_index("fy"), lax.axis_index("fz")
    ring_z, ring_y = ix // RING_Y, ix % RING_Y
    on_wall = iz == 0
    is_solver = iy == ix % NFY

    def owner_at(step):
        z = (ring_z + far_first(step // RING_Y, RING_Z)) % RING_Z
        y = (ring_y + far_first(step % RING_Y, RING_Y)) % RING_Y
        return z * RING_Y + y

    def face_at(step):
        z = (ring_z + far_first(step // 16, RING_Z)) % RING_Z
        y = (ring_y + far_first((step // 4) % 4, RING_Y)) % RING_Y
        return z * RING_Y + y, (iy + far_first(step % 4, NFY)) % NFY

    def signal(barrier, device):
        pl.semaphore_signal(barrier, inc=1, device_id=device, device_id_type=MESH)

    loads = [
        pltpu.make_async_copy(state_in, S.at[0, :, pl.ds(1, NZL)], load_sem.at[0]),
        pltpu.make_async_copy(kappa_in, K, load_sem.at[1]),
        pltpu.make_async_copy(inverse_in, BI, load_sem.at[2]),
        pltpu.make_async_copy(coupling_in, CO, load_sem.at[3]),
    ]
    for load in loads:
        load.start()
    XR[...] = jnp.zeros_like(XR)
    YR[...] = jnp.zeros_like(YR)
    zero_plane = jnp.zeros((NV, CX, CY), F32)
    for buffer in range(2):
        S[buffer, :, 0] = zero_plane
        S[buffer, :, NZL + 1] = zero_plane

    barrier = pltpu.get_barrier_semaphore()
    neighbours = (
        (ix > 0, (ix - 1, iy, iz)),
        (ix < NFX - 1, (ix + 1, iy, iz)),
        (iy > 0, (ix, iy - 1, iz)),
        (iy < NFY - 1, (ix, iy + 1, iz)),
    )

    @pl.when(is_solver)
    def _():
        def to_faces(step, carry):
            to_x, to_y = face_at(step)

            @pl.when(jnp.logical_not(jnp.logical_and(jnp.logical_and(to_x == ix, to_y == iy), on_wall)))
            def _():
                signal(barrier, (to_x, to_y, 0))

            return carry

        lax.fori_loop(0, NFX * NFY, to_faces, 0)

    def to_solvers(step, carry):
        to = owner_at(step)

        @pl.when(jnp.logical_not(jnp.logical_and(to == ix, is_solver)))
        def _():
            signal(barrier, (to, to % NFY, iz))

        return carry

    lax.fori_loop(0, NFX, to_solvers, 0)
    expected = jnp.int32(1)
    signal(barrier, (ix, iy, 1 - iz))
    for present, device in neighbours:
        expected = expected + present.astype(jnp.int32)

        @pl.when(present)
        def _():
            signal(barrier, device)

    solver_count = is_solver.astype(jnp.int32)
    wall_count = on_wall.astype(jnp.int32)
    expected = expected + wall_count * (2 * NFX - solver_count) + solver_count * (NFX * NFY - 1)

    rows = lax.broadcasted_iota(jnp.int32, (CAP * NFX, CX), 0)
    faces = lax.broadcasted_iota(jnp.int32, (CAP * NFX, CX), 1)
    named = (owner[...] == rows // CAP).astype(F32)
    earlier = (
        lax.broadcasted_iota(jnp.int32, (CX, CX), 0) < lax.broadcasted_iota(jnp.int32, (CX, CX), 1)
    ).astype(BF16)
    rank = jnp.dot(named.astype(BF16), earlier, preferred_element_type=F32)
    chosen = jnp.where(rank == (rows % CAP).astype(F32), named, 0.0)
    AM[...] = chosen
    unit = (lax.broadcasted_iota(jnp.int32, (CX, CX), 0) == lax.broadcasted_iota(jnp.int32, (CX, CX), 1)).astype(F32)
    AT[...] = lax.dot_general(unit, chosen, NT, preferred_element_type=F32)
    slot_rows = jnp.sum(chosen * (slot[...] + 1).astype(F32), axis=1, keepdims=True)
    SF[...] = jnp.broadcast_to(slot_rows, (CAP * NFX, CY))

    pl.semaphore_wait(barrier, expected)

    def send_to_solvers(turn):
        def send(step, carry):
            to = owner_at(step // 2)
            to_z = step % 2
            here = jnp.logical_and(jnp.logical_and(to == ix, is_solver), to_z == iz)
            source = SF.at[pl.ds(CAP * to, CAP)]
            target = RF.at[turn, pl.ds(CAP * (ix * NFY + iy), CAP)]

            @pl.when(here)
            def _():
                pltpu.make_async_copy(source, target, frecv.at[turn]).start()

            @pl.when(jnp.logical_not(here))
            def _():
                pltpu.make_async_remote_copy(
                    source, target, fsend.at[turn], frecv.at[turn], device_id=(to, to % NFY, to_z), device_id_type=MESH
                ).start()

            return carry

        @pl.when(on_wall)
        def _():
            lax.fori_loop(0, 2 * NFX, send, 0)

    def sent_to_solvers(turn):
        @pl.when(on_wall)
        def _():
            @pl.when(is_solver)
            def _():
                rest = RF.at[turn, pl.ds(0, CAP * (2 * NFX - 1))]
                pltpu.make_async_copy(rest, rest, fsend.at[turn]).wait()

            @pl.when(jnp.logical_not(is_solver))
            def _():
                rest = RF.at[turn, pl.ds(0, CAP * 2 * NFX)]
                pltpu.make_async_copy(rest, rest, fsend.at[turn]).wait()

    def heard_from_faces(turn):
        whole = RF.at[turn]
        pltpu.make_async_copy(whole, whole, frecv.at[turn]).wait()

    def send_to_faces(turn):
        def send(step, carry):
            to_x, to_y = face_at(step)
            here = jnp.logical_and(to_x == ix, to_y == iy)
            source = SD.at[pl.ds(CAP * (to_x * NFY + to_y), CAP)]
            target = RD.at[turn, pl.ds(CAP * ix, CAP)]

            @pl.when(here)
            def _():
                pltpu.make_async_copy(source, target, drecv.at[turn]).start()

            @pl.when(jnp.logical_not(here))
            def _():
                pltpu.make_async_remote_copy(
                    source, target, dsend.at[turn], drecv.at[turn], device_id=(to_x, to_y, iz), device_id_type=MESH
                ).start()

            return carry

        lax.fori_loop(0, NFX * NFY, send, 0)

    def sent_to_faces(turn):
        rest = RF.at[turn, pl.ds(0, FACES - CAP)]
        pltpu.make_async_copy(rest, rest, dsend.at[turn]).wait()

    send_to_solvers(ITERS)

    for load in loads:
        load.wait()

    @pl.when(is_solver)
    def _():
        def products(k, carry):
            block = order[0, k]
            inverse = BI[block]
            force_part = lax.dot_general(interp[...], inverse, NT, precision=HIGHEST, preferred_element_type=F32)
            chain = jnp.dot(inverse, CO[block], precision=HIGHEST, preferred_element_type=F32)
            high, low = split(jnp.concatenate([force_part, -chain.T], axis=0))
            R[k] = jnp.concatenate([high, low], axis=1)
            return carry

        lax.fori_loop(0, EBD, products, 0)

    sent_to_solvers(ITERS)

    block_rows = lax.broadcasted_iota(jnp.int32, (EBD, EB), 0)
    block_lanes = lax.broadcasted_iota(jnp.int32, (EBD, EB), 1)
    placed = jnp.zeros((EBD, EB), F32)
    for k in range(EBD):
        placed = jnp.where(jnp.logical_and(block_rows == k, block_lanes == order[0, k]), 1.0, placed)

    @pl.when(is_solver)
    def _():
        heard_from_faces(ITERS)
        face_lanes = lax.broadcasted_iota(jnp.int32, (FACES, EB), 1) + 1
        slot_of = (RF[ITERS] == face_lanes.astype(F32)).astype(F32)
        FP[...] = lax.dot_general(placed, slot_of, NT, preferred_element_type=F32)
        FPT[...] = lax.dot_general(slot_of, placed, NT, preferred_element_type=F32)

    lane = lax.broadcasted_iota(jnp.int32, (CX, CY), 1)
    row = lax.broadcasted_iota(jnp.int32, (CX, CY), 0)

    def pack(src):
        def plane(z, carry):
            low, high = carry
            for c in range(NV):
                centre = src[c, z + 1]
                XS[0, c, pl.ds(z, 1), :] = centre[0:1]
                XS[1, c, pl.ds(z, 1), :] = centre[CX - 1 : CX]
                here = lane == c * NZL + z
                low = jnp.where(here, centre[:, 0:1], low)
                high = jnp.where(here, centre[:, CY - 1 : CY], high)
            return low, high

        nothing = jnp.zeros((CX, CY), F32)
        low, high = lax.fori_loop(0, NZL, plane, (nothing, nothing))
        YS[0] = low
        YS[1] = high

    def halo_copies(n, src):
        def remote(source, target, at, there, device):
            return pltpu.make_async_remote_copy(
                source, target, hsend.at[n, at], hrecv.at[n, there], device_id=device, device_id_type=MESH
            )

        (has_left, left), (has_right, right), (has_front, front), (has_back, back) = neighbours
        always = iz >= 0
        sends = (
            (has_left, remote(XS.at[0], XR.at[n, 1], 0, 1, left)),
            (has_right, remote(XS.at[1], XR.at[n, 0], 1, 0, right)),
            (has_front, remote(YS.at[0], YR.at[n, 1], 2, 3, front)),
            (has_back, remote(YS.at[1], YR.at[n, 0], 3, 2, back)),
            (always, remote(src.at[:, NZL - (NZL - 1) * iz], ZR.at[n], 4, 4, (ix, iy, 1 - iz))),
        )
        waits = (
            (has_left, remote(XS.at[0], XR.at[n, 0], 0, 0, left)),
            (has_right, remote(XS.at[1], XR.at[n, 1], 1, 1, right)),
            (has_front, remote(YS.at[0], YR.at[n, 0], 2, 2, front)),
            (has_back, remote(YS.at[1], YR.at[n, 1], 3, 3, back)),
            (always, remote(src.at[:, NZL - (NZL - 1) * iz], ZR.at[n], 4, 4, (ix, iy, 1 - iz))),
        )
        return sends, waits

    def sweep(n, src, dst):
        pack(src)
        sends, waits = halo_copies(n, src)
        for present, copy in sends:

            @pl.when(present)
            def _():
                copy.start()

        for present, copy in waits:

            @pl.when(present)
            def _():
                copy.wait_recv()

        for present, copy in sends:

            @pl.when(present)
            def _():
                copy.wait_send()

        src[:, (NZL + 1) * (1 - iz)] = ZR[n]

        def plane(z, carry):
            coeff = DIFFUSION * K[z]
            centres = [src[c, z + 1] for c in range(NV)]
            for c in range(NV):
                centre = centres[c]
                at = c * NZL + z
                beside = src[c, z] + src[c, z + 2]
                beside += jnp.where(row == 0, XR[n, 0, c, pl.ds(z, 1), :], pltpu.roll(centre, 1, 0))
                beside += jnp.where(row == CX - 1, XR[n, 1, c, pl.ds(z, 1), :], pltpu.roll(centre, CX - 1, 0))
                front = pltpu.roll(YR[n, 0], (CY - at) % CY, 1)
                back = pltpu.roll(YR[n, 1], CY - 1 - at, 1)
                beside += jnp.where(lane == 0, front, pltpu.roll(centre, 1, 1))
                beside += jnp.where(lane == CY - 1, back, pltpu.roll(centre, CY - 1, 1))
                total = centre + coeff * (beside - 6.0 * centre)
                for d in range(NV):
                    total += mix[c, d] * centres[d]
                dst[c, z + 1] = total
            return carry

        lax.fori_loop(0, NZL, plane, 0)

    def solve():
        for k in range(EBD):
            force = FR[pl.ds(k, 1), :]
            previous = XV[pl.ds(k - 1, 1), :] if k else jnp.zeros((1, EB), F32)
            both = jnp.concatenate([force, previous], axis=1)
            high = both.astype(BF16).astype(F32)
            at = lax.broadcasted_iota(jnp.int32, (8, 2 * EB), 0)
            left = jnp.where(at == 0, high, jnp.where(at == 1, both - high, 0.0)).astype(BF16)
            result = jnp.dot(left, R[k], preferred_element_type=F32)
            summed = result[:, :EB] + result[:, EB:]
            XV[pl.ds(k, 1), :] = summed[0:1] + summed[1:2]

    total_z = NZL * lax.axis_size("fz")

    def iteration(it, carry):
        sweep(2 * it, S.at[0], S.at[1])
        sweep(2 * it + 1, S.at[1], S.at[0])

        @pl.when(on_wall)
        def _():
            pressure = press_weight[0] * S[0, 0, 1]
            for c in range(1, NV):
                pressure += press_weight[c] * S[0, c, 1]
            SF[...] = pick(AM[...].astype(BF16), pressure)

        send_to_solvers(it)

        @pl.when(is_solver)
        def _():
            heard_from_faces(it)
            FR[...] = pick(FP[...].astype(BF16), RF[it])
            solve()
            facing = lax.dot_general(XV[...], interp[...], NT, precision=HIGHEST, preferred_element_type=F32)
            SD[...] = pick(FPT[...].astype(BF16), facing)
            send_to_faces(it)

        whole = RD.at[it]
        pltpu.make_async_copy(whole, whole, drecv.at[it]).wait()
        wall = pick(AT[...].astype(BF16), RD[it])

        def add(z, carry):
            height = (iz * NZL + z).astype(F32)
            raised = (1.0 - height / total_z) * wall
            for c in range(NV):
                S[0, c, z + 1] += source_weight[c] * raised
            return carry

        lax.fori_loop(0, NZL, add, 0)
        sent_to_solvers(it)

        @pl.when(is_solver)
        def _():
            sent_to_faces(it)

        return carry

    lax.fori_loop(0, ITERS, iteration, 0)

    out = pltpu.make_async_copy(S.at[0, :, pl.ds(1, NZL)], state_out, load_sem.at[0])
    out.start()

    def disp_copy(t, source, target):
        return pltpu.make_async_remote_copy(
            source, target, osend.at[t], orecv, device_id=(ix, (iy + t) % NFY, iz), device_id_type=MESH
        )

    @pl.when(is_solver)
    def _():
        back = lax.dot_general(placed, XV[...], (((0,), (0,)), ((), ())), precision=HIGHEST, preferred_element_type=F32)
        DV[...] = back[:EBD]
        for t in range(1, NFY):
            disp_copy(t, DV, DR).start()
        DR[...] = back[:EBD]
        for t in range(1, NFY):
            disp_copy(t, DV, DR).wait_send()

    @pl.when(jnp.logical_not(is_solver))
    def _():
        disp_copy(1, DV, DR).wait_recv()

    disp_out[...] = DR[...]
    out.wait()


def on_device(
    state, kappa, mix, press_weight, source_weight, interp, block_inverse, coupling, front_order, face_owner, face_slot
):
    anywhere = pl.BlockSpec(memory_space=pl.ANY)
    smem = pl.BlockSpec(memory_space=pltpu.SMEM)
    vmem = pl.BlockSpec(memory_space=pltpu.VMEM)
    dma = pltpu.SemaphoreType.DMA
    sweeps = 2 * ITERS
    return pl.pallas_call(
        kernel,
        out_shape=(
            jax.ShapeDtypeStruct(state.shape, F32),
            jax.ShapeDtypeStruct((EBD, EB), F32),
        ),
        in_specs=[anywhere, anywhere, smem, smem, smem, vmem, anywhere, anywhere, smem, vmem, vmem],
        out_specs=(anywhere, vmem),
        scratch_shapes=[
            pltpu.VMEM((2, NV, NZL + 2, CX, CY), F32),
            pltpu.VMEM((NZL, CX, CY), F32),
            pltpu.VMEM((EBD, EB, EB), F32),
            pltpu.VMEM((EBD, EB, EB), F32),
            pltpu.VMEM((EBD, 2 * EB, 2 * EB), BF16),
            pltpu.VMEM((2, NV, NZL, CY), F32),
            pltpu.VMEM((sweeps, 2, NV, NZL, CY), F32),
            pltpu.VMEM((2, CX, CY), F32),
            pltpu.VMEM((sweeps, 2, CX, CY), F32),
            pltpu.VMEM((sweeps, NV, CX, CY), F32),
            pltpu.VMEM((CAP * NFX, CY), F32),
            pltpu.VMEM((ITERS + 1, FACES, CY), F32),
            pltpu.VMEM((FACES, CY), F32),
            pltpu.VMEM((ITERS, CAP * NFX, CY), F32),
            pltpu.VMEM((EBD, FACES), F32),
            pltpu.VMEM((FACES, EBD), F32),
            pltpu.VMEM((CAP * NFX, CX), F32),
            pltpu.VMEM((CX, CAP * NFX), F32),
            pltpu.VMEM((EBD, EB), F32),
            pltpu.VMEM((EBD, EB), F32),
            pltpu.VMEM((EBD, EB), F32),
            pltpu.VMEM((EBD, EB), F32),
            dma((4,)),
            dma((sweeps, 5)),
            dma((sweeps, 5)),
            dma((ITERS + 1,)),
            dma((ITERS + 1,)),
            dma((ITERS,)),
            dma((ITERS,)),
            dma((NFY,)),
            dma,
        ],
        compiler_params=pltpu.CompilerParams(
            collective_id=0, has_side_effects=True, vmem_limit_bytes=40 * 1024 * 1024
        ),
    )(
        state, kappa, mix, press_weight, source_weight, interp, block_inverse, coupling, front_order,
        face_owner.reshape(1, -1), face_slot.reshape(1, -1),
    )


def solution(mesh):
    return jax.shard_map(
        on_device,
        mesh=mesh,
        in_specs=(
            P(None, "fz", "fx", "fy"),
            P("fz", "fx", "fy"),
            P(),
            P(),
            P(),
            P(),
            P("fx", None, None),
            P("fx", None, None),
            P("fx", None),
            P(("fx", "fy"), None),
            P(("fx", "fy")),
        ),
        out_specs=(P(None, "fz", "fx", "fy"), P("fx", None)),
        check_vma=False,
    )
```

time: 752 us -> 149 us (0.20)
  the two profiles are of different devices: /device:TPU:8 before, /device:TPU:1 now
where the time goes in v1:
time: 149 us; the launch traced here: 147 us
  Pallas kernels  139 us (93%)
  local copies, waits for them, and re-layouts  8.08 us (5%)
    pallas_call x1, Pallas kernels, on_device(): pl.pallas_call(kernel, out_shape=(jax.ShapeDtypeStruct(state.shape, F32),...  139 us
    unnamed x24, local copies, waits for them, and re-layouts  8.08 us

profile of v1, /device:TPU:1, one launch (start us, length us, event | category | flops | bytes accessed | tf_op | source)
XLA Modules:
  0.0 147.4 jit_solution(14926684384683442206)
XLA Ops:
  0.6 0.0 copy-start.9
  0.6 0.0 copy-start.10
  0.7 0.0 copy-start.6
  0.7 0.0 copy-start.7
  0.7 0.0 copy-start.8
  0.7 0.6 copy-done.9
  1.3 0.0 copy-done.10
  1.3 0.0 copy-done.6
  1.3 0.0 copy-done.7
  1.3 0.0 copy-done.8
  1.4 0.0 copy-start
  1.4 1.2 copy-done
  2.6 0.0 copy-start.1
  2.6 1.2 copy-done.1
  3.8 0.0 copy-start.2
  3.8 1.1 copy-done.2
  4.9 0.0 copy-start.3
  4.9 0.9 copy-done.3
  5.8 0.0 copy-start.4
  5.8 0.8 copy-done.4
  6.6 0.7 copy-done.5
  7.3 138.6 %shard_map.122 = (f32[5,8,32,128]{3,2,1,0:T(8,128)S(1)}, f32[16,128]{1,0:T(8,128)S(1)}) custom-call(f32[5,8,32,128]{3,2,1,0:T(8,128)S(1)} %copy-done.2, f32[8,32,128]{2,1,0:T(8,128)S(1)} %copy-done.3, f32[5,5]{1,0:T(8,128)S(1)} %copy-done.5, f32[5]{0:T(128)S(1)} %copy-done.6, f32[5]{0:T(128)S(1)} %copy-done.7, f32[128,128]{1,0:T(8,128)S(1)} %copy-done.4, ...), custom_call_target="tpu_custom_call" | custom-call | tf_op jit(solution)/shard_map/pallas_call | solution.py:418
  146.0 0.8 copy.15
  146.8 0.6 copy.16
  (1 shorter events, 0.0 us)
Async XLA Ops:
  0.6 0.7 copy-start.9
  0.6 0.7 copy-start.10
  0.7 0.7 copy-start.6
  0.7 0.7 copy-start.7
  0.7 0.7 copy-start.8
  1.4 1.2 copy-start
  2.6 1.2 copy-start.1
  3.8 1.1 copy-start.2
  4.9 0.9 copy-start.3
  5.8 0.8 copy-start.4
  6.6 0.7 copy-start.5

commit v2 on v1

v2 whole, which is shorter than its diff:
```python
import jax
import jax.numpy as jnp
from jax import lax
from jax.experimental import pallas as pl
from jax.experimental.pallas import tpu as pltpu
from jax.sharding import PartitionSpec as P

ITERS = 3
DIFFUSION = 0.16
HIGHEST = lax.Precision.HIGHEST
MESH = pl.DeviceIdType.MESH
F32 = jnp.float32
BF16 = jnp.bfloat16

NV, NZL, CX, CY = 5, 8, 32, 128
NZ = 16
NFX, NFY = 32, 4
RING_Z, RING_Y = 8, 4
EB, EBD, CAP = 128, 16, 2
FACES = NFX * NFY * CAP
PAD = 8
CXE = CX + 2 * PAD
NT = (((1,), (1,)), ((), ()))
FAR_Y = (2, 1, 3, 0)


def far_first(step, ring):
    return ring // 2 + (1 - 2 * (step % 2)) * ((step + 1) // 2)


def split(values):
    high = values.astype(BF16)
    return high, (values - high.astype(F32)).astype(BF16)


def pick(selector, values):
    high, low = split(values)
    return jnp.dot(selector, high, preferred_element_type=F32) + jnp.dot(selector, low, preferred_element_type=F32)


def kernel(
    state_in, kappa_in, mix_in, press_in, source_in, interp_in, inverse_in, coupling_in, order_in, owner_in, slot_in,
    state_out, disp_out,
    mix, press_weight, source_weight, interp, order, owner, slot,
    S, K, KX, KE, BI, CO, R, XS, XR, YS, YR, YK, ZR, KZ, SL, SF, RF, SD, RD, FP, FPT, AM, AT, FR, XV, DV, DR,
    WN, LP, LE, QB, PB,
    load_sem, hsend, hrecv, fsend, frecv, dsend, drecv, osend, orecv, wsend, wrecv, rsend, rrecv,
):
    ix, iy, iz = lax.axis_index("fx"), lax.axis_index("fy"), lax.axis_index("fz")
    ring_z, ring_y = ix // RING_Y, ix % RING_Y
    on_wall = iz == 0
    off_wall = iz == 1
    is_solver = iy == ring_y
    not_solver = jnp.logical_not(is_solver)
    turned_y = {d: (ring_y + d) % RING_Y for d in FAR_Y}
    turned_x = {d: (iy + d) % NFY for d in FAR_Y}
    answer_x = ((iy + 2 - iz) % NFY, (iy + 3 * iz) % NFY)

    def row_base(step):
        return ((ring_z + far_first(step, RING_Z)) % RING_Z) * RING_Y

    def signal(barrier, device):
        pl.semaphore_signal(barrier, inc=1, device_id=device, device_id_type=MESH)

    loads = [
        pltpu.make_async_copy(source, target, load_sem.at[n])
        for n, (source, target) in enumerate(
            (
                (owner_in, owner),
                (slot_in, slot),
                (order_in, order),
                (kappa_in, K),
                (state_in, S.at[0, :, pl.ds(1, NZL)]),
                (inverse_in, BI),
                (coupling_in, CO),
                (interp_in, interp),
                (mix_in, mix),
                (press_in, press_weight),
                (source_in, source_weight),
            )
        )
    ]
    for load in loads:
        load.start()

    barrier = pltpu.get_barrier_semaphore()
    has_left, has_right, has_front, has_back = ix > 0, ix < NFX - 1, iy > 0, iy < NFY - 1
    sides = (
        (has_left, (ix - 1, iy, iz)),
        (has_right, (ix + 1, iy, iz)),
        (has_front, (ix, iy - 1, iz)),
        (has_back, (ix, iy + 1, iz)),
    )
    corners = (
        (jnp.logical_and(has_left, has_front), (ix - 1, iy - 1, iz)),
        (jnp.logical_and(has_left, has_back), (ix - 1, iy + 1, iz)),
        (jnp.logical_and(has_right, has_front), (ix + 1, iy - 1, iz)),
        (jnp.logical_and(has_right, has_back), (ix + 1, iy + 1, iz)),
    )
    other_core = (ix, iy, 1 - iz)

    @pl.when(is_solver)
    def _():
        def greet(step, carry):
            base = row_base(step)
            for dy in FAR_Y:
                for dx in FAR_Y:
                    signal(barrier, (base + turned_y[dy], turned_x[dx], 0))
            return carry

        lax.fori_loop(0, RING_Z - 1, greet, 0)
        for dy in FAR_Y:
            for dx in FAR_Y:
                if dy or dx:
                    signal(barrier, (ring_z * RING_Y + turned_y[dy], turned_x[dx], 0))

        @pl.when(off_wall)
        def _():
            signal(barrier, (ix, iy, 0))

    @pl.when(on_wall)
    def _():
        cores = {dy: (iy + turned_y[dy]) % 2 for dy in FAR_Y}

        def greet(step, carry):
            base = row_base(step)
            for dy in FAR_Y:
                signal(barrier, (base + turned_y[dy], turned_y[dy], cores[dy]))
            return carry

        lax.fori_loop(0, RING_Z - 1, greet, 0)
        for dy in FAR_Y[:3]:
            signal(barrier, (ring_z * RING_Y + turned_y[dy], turned_y[dy], cores[dy]))

        @pl.when(not_solver)
        def _():
            signal(barrier, (ix, ring_y, cores[0]))

    @pl.when(not_solver)
    def _():
        signal(barrier, (ix, ring_y, iz))

    for ref in (XR, YR, WN):
        ref[...] = jnp.zeros_like(ref)

    signal(barrier, other_core)
    solver_count = is_solver.astype(jnp.int32)
    wall_count = on_wall.astype(jnp.int32)
    expected = 1 + wall_count * (2 * NFX - solver_count) + solver_count * (2 * NFX - wall_count + NFY - 1)
    for present, device in sides + corners:
        expected = expected + present.astype(jnp.int32)

        @pl.when(present)
        def _():
            signal(barrier, device)

    zero_plane = jnp.zeros((NV, CX, CY), F32)
    for buffer in range(2):
        S[buffer, :, 0] = zero_plane
        S[buffer, :, NZL + 1] = zero_plane

    for load in loads[:3]:
        load.wait()
    rows = lax.broadcasted_iota(jnp.int32, (CAP * NFX, CX), 0)
    named = (owner[...] == rows // CAP).astype(F32)
    earlier = (
        lax.broadcasted_iota(jnp.int32, (CX, CX), 0) < lax.broadcasted_iota(jnp.int32, (CX, CX), 1)
    ).astype(BF16)
    rank = jnp.dot(named.astype(BF16), earlier, preferred_element_type=F32)
    chosen = jnp.where(rank == (rows % CAP).astype(F32), named, 0.0)
    AM[...] = chosen
    unit = (lax.broadcasted_iota(jnp.int32, (CX, CX), 0) == lax.broadcasted_iota(jnp.int32, (CX, CX), 1)).astype(F32)
    AT[...] = lax.dot_general(unit, chosen, NT, preferred_element_type=F32)
    slot_rows = jnp.sum(chosen * (slot[...] + 1).astype(F32), axis=1, keepdims=True)
    SL[...] = jnp.broadcast_to(slot_rows, (CAP * NFX, CY))
    block_rows = lax.broadcasted_iota(jnp.int32, (EBD, EB), 0)
    block_lanes = lax.broadcasted_iota(jnp.int32, (EBD, EB), 1)
    placed = jnp.zeros((EBD, EB), F32)
    for k in range(EBD):
        placed = jnp.where(jnp.logical_and(block_rows == k, block_lanes == order[0, k]), 1.0, placed)

    lane = lax.broadcasted_iota(jnp.int32, (CX, CY), 1)
    row = lax.broadcasted_iota(jnp.int32, (CX, CY), 0)
    for load in loads[3:5]:
        load.wait()

    def kappa_faces(z, carry):
        low, high = carry
        coeff = DIFFUSION * K[z]
        KX[z + 1, PAD : PAD + CX] = coeff
        XS[0, NV, pl.ds(z, 1), :] = coeff[0:1]
        XS[1, NV, pl.ds(z, 1), :] = coeff[CX - 1 : CX]
        here = lane == NV * NZL + z
        return jnp.where(here, coeff[:, 0:1], low), jnp.where(here, coeff[:, CY - 1 : CY], high)

    nothing = jnp.zeros((CX, CY), F32)
    YK[0], YK[1] = lax.fori_loop(0, NZL, kappa_faces, (nothing, nothing))

    def pack(src):
        def plane(z, carry):
            low, high = carry
            for c in range(NV):
                centre = src[c, z + 1]
                XS[0, c, pl.ds(z, 1), :] = centre[0:1]
                XS[1, c, pl.ds(z, 1), :] = centre[CX - 1 : CX]
                here = lane == c * NZL + z
                low = jnp.where(here, centre[:, 0:1], low)
                high = jnp.where(here, centre[:, CY - 1 : CY], high)
            return low, high

        YS[0], YS[1] = lax.fori_loop(0, NZL, plane, (YK[0], YK[1]))

    edge = NZL - (NZL - 1) * iz

    def halo_copies(n, src):
        def remote(source, target, at, there, device):
            return pltpu.make_async_remote_copy(
                source, target, hsend.at[n, at], hrecv.at[n, there], device_id=device, device_id_type=MESH
            )

        (_, left), (_, right), (_, front), (_, back) = sides
        always = iz >= 0
        plane = src.at[:, edge]
        sends = (
            (has_left, remote(XS.at[0], XR.at[n, 1], 0, 1, left)),
            (has_right, remote(XS.at[1], XR.at[n, 0], 1, 0, right)),
            (has_front, remote(YS.at[0], YR.at[n, 1], 2, 3, front)),
            (has_back, remote(YS.at[1], YR.at[n, 0], 3, 2, back)),
            (always, remote(plane, ZR.at[n], 4, 4, other_core)),
        )
        waits = (
            (has_left, remote(XS.at[0], XR.at[n, 0], 0, 0, left)),
            (has_right, remote(XS.at[1], XR.at[n, 1], 1, 1, right)),
            (has_front, remote(YS.at[0], YR.at[n, 0], 2, 2, front)),
            (has_back, remote(YS.at[1], YR.at[n, 1], 3, 3, back)),
            (always, remote(plane, ZR.at[n], 4, 4, other_core)),
        )
        return sends, waits

    def each(copies, action):
        for present, copy in copies:

            @pl.when(present)
            def _():
                action(copy)

    def start_halo(n, src):
        pack(src)
        each(halo_copies(n, src)[0], lambda copy: copy.start())

    def finish_halo(n, src):
        sends, waits = halo_copies(n, src)
        each(waits, lambda copy: copy.wait_recv())
        each(sends, lambda copy: copy.wait_send())
        src[:, (NZL + 1) * (1 - iz)] = ZR[n]

    def sweep(n, src, dst):
        def plane(z, carry):
            coeff = KX[z + 1, PAD : PAD + CX]
            centres = [src[c, z + 1] for c in range(NV)]
            for c in range(NV):
                centre = centres[c]
                at = c * NZL + z
                beside = src[c, z] + src[c, z + 2]
                beside += jnp.where(row == 0, XR[n, 0, c, pl.ds(z, 1), :], pltpu.roll(centre, 1, 0))
                beside += jnp.where(row == CX - 1, XR[n, 1, c, pl.ds(z, 1), :], pltpu.roll(centre, CX - 1, 0))
                front = pltpu.roll(YR[n, 0], (CY - at) % CY, 1)
                back = pltpu.roll(YR[n, 1], CY - 1 - at, 1)
                beside += jnp.where(lane == 0, front, pltpu.roll(centre, 1, 1))
                beside += jnp.where(lane == CY - 1, back, pltpu.roll(centre, CY - 1, 1))
                total = centre + coeff * (beside - 6.0 * centre)
                for d in range(NV):
                    total += mix[c, d] * centres[d]
                dst[c, z + 1] = total
            return carry

        lax.fori_loop(0, NZL, plane, 0)

    kappa_plane = pltpu.make_async_remote_copy(
        KX.at[edge], KZ, osend.at[0], orecv.at[0], device_id=other_core, device_id_type=MESH
    )

    def send_to_solvers(turn, rows_out):
        target = RF.at[turn, pl.ds(CAP * (ix * NFY + iy), CAP)]

        def send(to, y, core):
            pltpu.make_async_remote_copy(
                rows_out.at[pl.ds(CAP * to, CAP)], target, fsend.at[turn], frecv.at[turn],
                device_id=(to, y, core), device_id_type=MESH,
            ).start()

        def group(step, carry):
            base = row_base(step)
            for dy in FAR_Y:
                for core in range(2):
                    send(base + turned_y[dy], turned_y[dy], core)
            return carry

        @pl.when(on_wall)
        def _():
            lax.fori_loop(0, RING_Z - 1, group, 0)
            for dy in FAR_Y[:3]:
                for core in range(2):
                    send(ring_z * RING_Y + turned_y[dy], turned_y[dy], core)
            send(ix, ring_y, 1)

            @pl.when(not_solver)
            def _():
                send(ix, ring_y, 0)

            @pl.when(is_solver)
            def _():
                pltpu.make_async_copy(rows_out.at[pl.ds(CAP * ix, CAP)], target, frecv.at[turn]).start()

    def sent_to_solvers(turn):
        @pl.when(on_wall)
        def _():
            @pl.when(is_solver)
            def _():
                rest = RF.at[turn, pl.ds(0, CAP * (2 * NFX - 1))]
                pltpu.make_async_copy(rest, rest, fsend.at[turn]).wait()

            @pl.when(not_solver)
            def _():
                rest = RF.at[turn, pl.ds(0, CAP * 2 * NFX)]
                pltpu.make_async_copy(rest, rest, fsend.at[turn]).wait()

    def heard_from_faces(turn):
        whole = RF.at[turn]
        pltpu.make_async_copy(whole, whole, frecv.at[turn]).wait()

    def send_to_faces(turn):
        target = RD.at[turn, pl.ds(CAP * ix, CAP)]

        def send(to_x, to_y):
            pltpu.make_async_remote_copy(
                SD.at[pl.ds(CAP * (to_x * NFY + to_y), CAP)], target, dsend.at[turn], drecv.at[turn],
                device_id=(to_x, to_y, 0), device_id_type=MESH,
            ).start()

        def group(step, carry):
            base = row_base(step)
            for dy in FAR_Y:
                for x in answer_x:
                    send(base + turned_y[dy], x)
            return carry

        lax.fori_loop(0, RING_Z - 1, group, 0)
        for dy in FAR_Y[:3]:
            for x in answer_x:
                send(ring_z * RING_Y + turned_y[dy], x)
        send(ix, answer_x[0])

        @pl.when(off_wall)
        def _():
            send(ix, answer_x[1])

        @pl.when(on_wall)
        def _():
            pltpu.make_async_copy(SD.at[pl.ds(CAP * (ix * NFY + iy), CAP)], target, drecv.at[turn]).start()

    def sent_to_faces(turn):
        @pl.when(on_wall)
        def _():
            rest = RF.at[turn, pl.ds(0, CAP * (2 * NFX - 1))]
            pltpu.make_async_copy(rest, rest, dsend.at[turn]).wait()

        @pl.when(off_wall)
        def _():
            rest = RF.at[turn, pl.ds(0, CAP * 2 * NFX)]
            pltpu.make_async_copy(rest, rest, dsend.at[turn]).wait()

    for load in loads[5:]:
        load.wait()

    @pl.when(is_solver)
    def _():
        def products(k, carry):
            block = order[0, k]
            inverse = BI[block]
            force_part = lax.dot_general(interp[...], inverse, NT, precision=HIGHEST, preferred_element_type=F32)
            chain = jnp.dot(inverse, CO[block], precision=HIGHEST, preferred_element_type=F32)
            high, low = split(jnp.concatenate([force_part, -chain.T], axis=0))
            R[k] = jnp.concatenate([high, low], axis=1)
            return carry

        lax.fori_loop(0, EBD, products, 0)

    numbers = range(NV)
    source = [source_weight[c] for c in numbers]
    once = [source[c] + sum(mix[c, d] * source[d] for d in numbers) for c in numbers]
    twice = [once[c] + sum(mix[c, d] * once[d] for d in numbers) for c in numbers]
    press_source = sum(press_weight[c] * source[c] for c in numbers)
    press_once = sum(press_weight[c] * once[c] for c in numbers)
    press_twice = sum(press_weight[c] * twice[c] for c in numbers)

    pl.semaphore_wait(barrier, expected)
    start_halo(0, S.at[0])
    kappa_plane.start()
    send_to_solvers(ITERS, SL)
    finish_halo(0, S.at[0])
    sweep(0, S.at[0], S.at[1])
    start_halo(1, S.at[1])

    kappa_plane.wait()
    KX[(NZL + 1) * (1 - iz)] = KZ[...]
    KX[(NZL + 1) * iz] = jnp.zeros((CXE, CY), F32)
    tile_row = lax.broadcasted_iota(jnp.int32, (PAD, CY), 0)

    def kappa_edges(z, carry):
        KX[z + 1, 0:PAD] = jnp.where(tile_row == PAD - 1, XR[0, 0, NV, pl.ds(z, 1), :], 0.0)
        KX[z + 1, PAD + CX : CXE] = jnp.where(tile_row == 0, XR[0, 1, NV, pl.ds(z, 1), :], 0.0)
        at = NV * NZL + z
        front = pltpu.roll(YR[0, 0], CY - 1 - at, 1)
        back = pltpu.roll(YR[0, 1], (CY - at) % CY, 1)
        KE[z] = jnp.where(lane >= CY // 2, front, back)
        return carry

    lax.fori_loop(0, NZL, kappa_edges, 0)

    def wall_base():
        @pl.when(on_wall)
        def _():
            pressure = press_weight[0] * S[0, 0, 1]
            for c in range(1, NV):
                pressure += press_weight[c] * S[0, c, 1]
            PB[...] = pressure

    finish_halo(1, S.at[1])
    sweep(1, S.at[1], S.at[0])
    wall_base()
    sent_to_solvers(ITERS)

    @pl.when(on_wall)
    def _():
        SF[...] = pick(AM[...].astype(BF16), PB[...])

    send_to_solvers(0, SF)

    @pl.when(is_solver)
    def _():
        heard_from_faces(ITERS)
        face_lanes = lax.broadcasted_iota(jnp.int32, (FACES, EB), 1) + 1
        slot_of = (RF[ITERS] == face_lanes.astype(F32)).astype(F32)
        FP[...] = lax.dot_general(placed, slot_of, NT, preferred_element_type=F32)
        FPT[...] = lax.dot_general(slot_of, placed, NT, preferred_element_type=F32)

    def solve():
        for k in range(EBD):
            force = FR[pl.ds(k, 1), :]
            previous = XV[pl.ds(k - 1, 1), :] if k else jnp.zeros((1, EB), F32)
            both = jnp.concatenate([force, previous], axis=1)
            high = both.astype(BF16).astype(F32)
            at = lax.broadcasted_iota(jnp.int32, (8, 2 * EB), 0)
            left = jnp.where(at == 0, high, jnp.where(at == 1, both - high, 0.0)).astype(BF16)
            result = jnp.dot(left, R[k], preferred_element_type=F32)
            summed = result[:, :EB] + result[:, EB:]
            XV[pl.ds(k, 1), :] = summed[0:1] + summed[1:2]

    def wall_copies(it):
        def remote(n, opposite, source_row, side, target_row, count, device):
            copy = lambda here, there: pltpu.make_async_remote_copy(
                WN.at[it, 1, pl.ds(source_row, count)], WN.at[it, side, pl.ds(target_row, count)],
                wsend.at[it, here], wrecv.at[it, there], device_id=device, device_id_type=MESH,
            )
            return copy(n, opposite), copy(n, n)

        low, high = PAD, PAD + CX - 8
        (_, left), (_, right), (_, front), (_, back) = sides
        (lf, left_front), (lb, left_back), (rf, right_front), (rb, right_back) = corners
        return (
            (has_left, remote(0, 1, low, 1, PAD + CX, 8, left)),
            (has_right, remote(1, 0, high, 1, 0, 8, right)),
            (has_front, remote(2, 3, PAD, 2, PAD, CX, front)),
            (has_back, remote(3, 2, PAD, 0, PAD, CX, back)),
            (lf, remote(4, 7, low, 2, PAD + CX, 8, left_front)),
            (lb, remote(5, 6, low, 0, PAD + CX, 8, left_back)),
            (rf, remote(6, 5, high, 2, 0, 8, right_front)),
            (rb, remote(7, 4, high, 0, 0, 8, right_back)),
        )

    lane_e = lax.broadcasted_iota(jnp.int32, (CXE, CY), 1)
    inner = slice(PAD, PAD + CX)

    def spread(it):
        centre = WN[it, 1]
        beyond = jnp.where(lane_e >= CY // 2, WN[it, 0], WN[it, 2])
        up, down = pltpu.roll(centre, 1, 1), pltpu.roll(centre, CY - 1, 1)
        out_up, out_down = pltpu.roll(beyond, 1, 1), pltpu.roll(beyond, CY - 1, 1)
        lap = pltpu.roll(centre, 1, 0) + pltpu.roll(centre, CXE - 1, 0) - 4.0 * centre
        lap += jnp.where(lane_e == 0, out_up, up) + jnp.where(lane_e == CY - 1, out_down, down)
        lap_e = pltpu.roll(beyond, 1, 0) + pltpu.roll(beyond, CXE - 1, 0) - 4.0 * beyond
        lap_e += jnp.where(lane_e >= CY // 2, out_up + down, out_down + up)
        LP[0], LP[1] = lap, centre
        LE[0], LE[1] = lap_e[inner], beyond[inner]

    def ring_sum(wide, edge_columns, below, above, coeff):
        own = wide[inner]
        total = pltpu.roll(wide, 1, 0)[inner] + pltpu.roll(wide, CXE - 1, 0)[inner] + below + above - 6.0 * own
        total += jnp.where(lane == 0, pltpu.roll(edge_columns, 1, 1), pltpu.roll(own, 1, 1))
        total += jnp.where(lane == CY - 1, pltpu.roll(edge_columns, CY - 1, 1), pltpu.roll(own, CY - 1, 1))
        return coeff * total

    first_jump = (NZ - 1.0) / NZ - 2.0

    def wall_response(it):
        wide = KX[1] * (LP[0] + first_jump * LP[1])
        edges = KE[0] * (LE[0] + first_jump * LE[1])
        above = KX[2, inner] * ((NZ - 1.0) / NZ * LP[0, inner])
        bend = ring_sum(wide, edges, 0.0, above, KX[1, inner])
        return press_twice * LP[1, inner] + 2.0 * press_once * wide[inner] + press_source * bend

    def profile(plane):
        height = iz * NZL + plane - 1
        return 1.0 - height.astype(F32) / NZ, jnp.where(height == 0, first_jump, 0.0)

    def update():
        def first(plane, carry):
            share, jump = profile(plane)
            QB[plane] = KX[plane] * (share * LP[0] + jump * LP[1])
            return carry

        lax.fori_loop(0, NZL + 2, first, 0)

        def second(z, carry):
            share, jump = profile(z + 1)
            edges = KE[z] * (share * LE[0] + jump * LE[1])
            wide = QB[z + 1]
            bend = ring_sum(wide, edges, QB[z, inner], QB[z + 2, inner], KX[z + 1, inner])
            raised, slope = share * LP[1, inner], wide[inner]
            for c in range(NV):
                S[0, c, z + 1] += twice[c] * raised + 2.0 * once[c] * slope + source[c] * bend
            return carry

        lax.fori_loop(0, NZL, second, 0)

    def iteration(it, carry):
        more = it < ITERS - 1
        n = 2 * it + 2

        @pl.when(more)
        def _():
            start_halo(n, S.at[0])
            finish_halo(n, S.at[0])
            sweep(n, S.at[0], S.at[1])
            start_halo(n + 1, S.at[1])

        @pl.when(is_solver)
        def _():
            heard_from_faces(it)
            FR[...] = pick(FP[...].astype(BF16), RF[it])
            solve()
            facing = lax.dot_general(XV[...], interp[...], NT, precision=HIGHEST, preferred_element_type=F32)
            SD[...] = pick(FPT[...].astype(BF16), facing)
            send_to_faces(it)

        @pl.when(more)
        def _():
            finish_halo(n + 1, S.at[1])
            sweep(n + 1, S.at[1], S.at[0])
            wall_base()

        relay = pltpu.make_async_remote_copy(
            WN.at[it], WN.at[it], rsend.at[it], rrecv.at[it], device_id=other_core, device_id_type=MESH
        )

        @pl.when(on_wall)
        def _():
            sent_to_solvers(it)
            whole = RD.at[it]
            pltpu.make_async_copy(whole, whole, drecv.at[it]).wait()
            WN[it, 1, inner] = pick(AT[...].astype(BF16), RD[it])

            @pl.when(more)
            def _():
                copies = wall_copies(it)
                each(copies, lambda pair: pair[0].start())
                each(copies, lambda pair: pair[1].wait_recv())
                spread(it)
                SF[...] = pick(AM[...].astype(BF16), PB[...] + wall_response(it))
                send_to_solvers(it + 1, SF)
                each(copies, lambda pair: pair[0].wait_send())

            relay.start()

        @pl.when(off_wall)
        def _():
            relay.wait_recv()

        @pl.when(more)
        def _():
            @pl.when(off_wall)
            def _():
                spread(it)

            update()

        @pl.when(on_wall)
        def _():
            relay.wait_send()

        @pl.when(is_solver)
        def _():
            sent_to_faces(it)

        return carry

    lax.fori_loop(0, ITERS, iteration, 0)

    wall = WN[ITERS - 1, 1, inner]

    def add(z, carry):
        share, _ = profile(z + 1)
        raised = share * wall
        for c in range(NV):
            S[0, c, z + 1] += source[c] * raised
        return carry

    lax.fori_loop(0, NZL, add, 0)
    out = pltpu.make_async_copy(S.at[0, :, pl.ds(1, NZL)], state_out, load_sem.at[0])
    out.start()

    def disp_copy(t):
        return pltpu.make_async_remote_copy(
            DV, DR, osend.at[t], orecv.at[1], device_id=(ix, (iy + t) % NFY, iz), device_id_type=MESH
        )

    @pl.when(is_solver)
    def _():
        back = lax.dot_general(placed, XV[...], (((0,), (0,)), ((), ())), precision=HIGHEST, preferred_element_type=F32)
        DV[...] = back[:EBD]
        for t in range(1, NFY):
            disp_copy(t).start()
        DR[...] = back[:EBD]
        for t in range(1, NFY):
            disp_copy(t).wait_send()

    @pl.when(not_solver)
    def _():
        disp_copy(1).wait_recv()

    disp_out[...] = DR[...]
    out.wait()


def on_device(
    state, kappa, mix, press_weight, source_weight, interp, block_inverse, coupling, front_order, face_owner, face_slot
):
    hbm = pl.BlockSpec(memory_space=pltpu.HBM)
    vmem = pl.BlockSpec(memory_space=pltpu.VMEM)
    dma = pltpu.SemaphoreType.DMA
    sweeps = 2 * ITERS
    return pl.pallas_call(
        kernel,
        out_shape=(
            jax.ShapeDtypeStruct(state.shape, F32),
            jax.ShapeDtypeStruct((EBD, EB), F32),
        ),
        in_specs=[hbm] * 11,
        out_specs=(hbm, vmem),
        scratch_shapes=[
            pltpu.SMEM((NV, NV), F32),
            pltpu.SMEM((NV,), F32),
            pltpu.SMEM((NV,), F32),
            pltpu.VMEM((CY, EB), F32),
            pltpu.SMEM((1, EBD), jnp.int32),
            pltpu.VMEM((1, CX), jnp.int32),
            pltpu.VMEM((1, CX), jnp.int32),
            pltpu.VMEM((2, NV, NZL + 2, CX, CY), F32),
            pltpu.VMEM((NZL, CX, CY), F32),
            pltpu.VMEM((NZL + 2, CXE, CY), F32),
            pltpu.VMEM((NZL, CX, CY), F32),
            pltpu.VMEM((EBD, EB, EB), F32),
            pltpu.VMEM((EBD, EB, EB), F32),
            pltpu.VMEM((EBD, 2 * EB, 2 * EB), BF16),
            pltpu.VMEM((2, NV + 1, NZL, CY), F32),
            pltpu.VMEM((sweeps, 2, NV + 1, NZL, CY), F32),
            pltpu.VMEM((2, CX, CY), F32),
            pltpu.VMEM((sweeps, 2, CX, CY), F32),
            pltpu.VMEM((2, CX, CY), F32),
            pltpu.VMEM((sweeps, NV, CX, CY), F32),
            pltpu.VMEM((CXE, CY), F32),
            pltpu.VMEM((CAP * NFX, CY), F32),
            pltpu.VMEM((CAP * NFX, CY), F32),
            pltpu.VMEM((ITERS + 1, FACES, CY), F32),
            pltpu.VMEM((FACES, CY), F32),
            pltpu.VMEM((ITERS, CAP * NFX, CY), F32),
            pltpu.VMEM((EBD, FACES), F32),
            pltpu.VMEM((FACES, EBD), F32),
            pltpu.VMEM((CAP * NFX, CX), F32),
            pltpu.VMEM((CX, CAP * NFX), F32),
            pltpu.VMEM((EBD, EB), F32),
            pltpu.VMEM((EBD, EB), F32),
            pltpu.VMEM((EBD, EB), F32),
            pltpu.VMEM((EBD, EB), F32),
            pltpu.VMEM((ITERS, 3, CXE, CY), F32),
            pltpu.VMEM((2, CXE, CY), F32),
            pltpu.VMEM((2, CX, CY), F32),
            pltpu.VMEM((NZL + 2, CXE, CY), F32),
            pltpu.VMEM((CX, CY), F32),
            dma((11,)),
            dma((sweeps, 5)),
            dma((sweeps, 5)),
            dma((ITERS + 1,)),
            dma((ITERS + 1,)),
            dma((ITERS,)),
            dma((ITERS,)),
            dma((NFY,)),
            dma((2,)),
            dma((ITERS, 8)),
            dma((ITERS, 8)),
            dma((ITERS,)),
            dma((ITERS,)),
        ],
        compiler_params=pltpu.CompilerParams(
            collective_id=0, has_side_effects=True, vmem_limit_bytes=40 * 1024 * 1024
        ),
    )(
        state, kappa, mix, press_weight, source_weight, interp, block_inverse, coupling, front_order,
        face_owner.reshape(1, -1), face_slot.reshape(1, -1),
    )


def solution(mesh):
    return jax.shard_map(
        on_device,
        mesh=mesh,
        in_specs=(
            P(None, "fz", "fx", "fy"),
            P("fz", "fx", "fy"),
            P(),
            P(),
            P(),
            P(),
            P("fx", None, None),
            P("fx", None, None),
            P("fx", None),
            P(("fx", "fy"), None),
            P(("fx", "fy")),
        ),
        out_specs=(P(None, "fz", "fx", "fy"), P("fx", None)),
        check_vma=False,
    )
```

time: 149 us -> 102 us (0.68)
  Pallas kernels: 139 us -> 92.7 us
    pallas_call x1, Pallas kernels: 139 us -> 92.7 us  [on_device(): pl.pallas_call(kernel, out_shape=(jax.ShapeDtypeStruct(state.shape, F32),...]
where the time goes in v2:
time: 102 us; the launch traced here: 101 us
  Pallas kernels  92.7 us (91%)
  local copies, waits for them, and re-layouts  8.08 us (8%)
    pallas_call x1, Pallas kernels, on_device(): pl.pallas_call(kernel, out_shape=(jax.ShapeDtypeStruct(state.shape, F32),...  92.7 us
    unnamed x24, local copies, waits for them, and re-layouts  8.08 us

profile of v2, /device:TPU:1, one launch (start us, length us, event | category | flops | bytes accessed | tf_op | source)
XLA Modules:
  0.0 101.4 jit_solution(17044102749629205395)
XLA Ops:
  0.6 0.0 copy-start.9
  0.6 0.0 copy-start.10
  0.7 0.0 copy-start.6
  0.7 0.0 copy-start.7
  0.7 0.0 copy-start.8
  0.7 0.6 copy-done.9
  1.3 0.0 copy-done.10
  1.3 0.0 copy-done.6
  1.3 0.0 copy-done.7
  1.3 0.0 copy-done.8
  1.4 0.0 copy-start
  1.4 1.2 %copy-done = f32[16,128,128]{2,1,0:T(8,128)S(1)} copy-done((f32[16,128,128]{2,1,0:T(8,128)S(1)}, f32[16,128,128]{2,1,0:T(8,128)}, u32[]{:S(2)}) %copy-start) | copy-done | bytes 1048600
  2.6 0.0 copy-start.1
  2.6 1.2 %copy-done.1 = f32[16,128,128]{2,1,0:T(8,128)S(1)} copy-done((f32[16,128,128]{2,1,0:T(8,128)S(1)}, f32[16,128,128]{2,1,0:T(8,128)}, u32[]{:S(2)}) %copy-start.1) | copy-done | bytes 1048600
  3.8 0.0 copy-start.2
  3.8 1.1 %copy-done.2 = f32[5,8,32,128]{3,2,1,0:T(8,128)S(1)} copy-done((f32[5,8,32,128]{3,2,1,0:T(8,128)S(1)}, f32[5,8,32,128]{3,2,1,0:T(8,128)}, u32[]{:S(2)}) %copy-start.2) | copy-done | bytes 655384
  4.9 0.0 copy-start.3
  4.9 0.9 copy-done.3
  5.8 0.0 copy-start.4
  5.8 0.8 copy-done.4
  6.6 0.7 copy-done.5
  7.3 92.7 %shard_map.122 = (f32[5,8,32,128]{3,2,1,0:T(8,128)S(1)}, f32[16,128]{1,0:T(8,128)S(1)}) custom-call(f32[5,8,32,128]{3,2,1,0:T(8,128)S(1)} %copy-done.2, f32[8,32,128]{2,1,0:T(8,128)S(1)} %copy-done.3, f32[5,5]{1,0:T(8,128)S(1)} %copy-done.5, f32[5]{0:T(128)S(1)} %copy-done.6, f32[5]{0:T(128)S(1)} %copy-done.7, f32[128,128]{1,0:T(8,128)S(1)} %copy-done.4, ...), custom_call_target="tpu_custom_call" | custom-call | tf_op jit(solution)/shard_map/pallas_call | solution.py:653
  100.0 0.8 copy.15
  100.8 0.6 copy.16
  (1 shorter events, 0.0 us)
Async XLA Ops:
  0.6 0.7 copy-start.9
  0.6 0.7 copy-start.10
  0.7 0.7 copy-start.6
  0.7 0.7 copy-start.7
  0.7 0.7 copy-start.8
  1.4 1.2 %copy-start = (f32[16,128,128]{2,1,0:T(8,128)S(1)}, f32[16,128,128]{2,1,0:T(8,128)}, u32[]{:S(2)}) copy-start(f32[16,128,128]{2,1,0:T(8,128)} %inverse_in.1) | copy-start | bytes 3145732
  2.6 1.2 %copy-start.1 = (f32[16,128,128]{2,1,0:T(8,128)S(1)}, f32[16,128,128]{2,1,0:T(8,128)}, u32[]{:S(2)}) copy-start(f32[16,128,128]{2,1,0:T(8,128)} %coupling_in.1) | copy-start | bytes 3145732
  3.8 1.1 %copy-start.2 = (f32[5,8,32,128]{3,2,1,0:T(8,128)S(1)}, f32[5,8,32,128]{3,2,1,0:T(8,128)}, u32[]{:S(2)}) copy-start(f32[5,8,32,128]{3,2,1,0:T(8,128)} %state_in.1) | copy-start | bytes 1966084
  4.9 0.9 copy-start.3
  5.8 0.8 copy-start.4
  6.6 0.7 copy-start.5

commit v3 on v2

--- a/solution.py
+++ b/solution.py
@@ -40,7 +40,7 @@
 
 def kernel(
     state_in, kappa_in, mix_in, press_in, source_in, interp_in, inverse_in, coupling_in, order_in, owner_in, slot_in,
-    state_out, disp_out,
+    state_out, raised_out, disp_out,
     mix, press_weight, source_weight, interp, order, owner, slot,
     S, K, KX, KE, BI, CO, R, XS, XR, YS, YR, YK, ZR, KZ, SL, SF, RF, SD, RD, FP, FPT, AM, AT, FR, XV, DV, DR,
     WN, LP, LE, QB, PB,
@@ -245,7 +245,6 @@
                 action(copy)
 
     def start_halo(n, src):
-        pack(src)
         each(halo_copies(n, src)[0], lambda copy: copy.start())
 
     def finish_halo(n, src):
@@ -394,12 +393,14 @@
     press_once = sum(press_weight[c] * once[c] for c in numbers)
     press_twice = sum(press_weight[c] * twice[c] for c in numbers)
 
+    pack(S.at[0])
     pl.semaphore_wait(barrier, expected)
     start_halo(0, S.at[0])
     kappa_plane.start()
     send_to_solvers(ITERS, SL)
     finish_halo(0, S.at[0])
     sweep(0, S.at[0], S.at[1])
+    pack(S.at[1])
     start_halo(1, S.at[1])
 
     kappa_plane.wait()
@@ -534,70 +535,65 @@
 
         lax.fori_loop(0, NZL, second, 0)
 
+    def answer(it):
+        heard_from_faces(it)
+        FR[...] = pick(FP[...].astype(BF16), RF[it])
+        solve()
+        facing = lax.dot_general(XV[...], interp[...], NT, precision=HIGHEST, preferred_element_type=F32)
+        SD[...] = pick(FPT[...].astype(BF16), facing)
+        send_to_faces(it)
+
+    def hear_wall(it):
+        sent_to_solvers(it)
+        whole = RD.at[it]
+        pltpu.make_async_copy(whole, whole, drecv.at[it]).wait()
+        WN[it, 1, inner] = pick(AT[...].astype(BF16), RD[it])
+
+    def relay(it, part):
+        return pltpu.make_async_remote_copy(
+            part, part, rsend.at[it], rrecv.at[it], device_id=other_core, device_id_type=MESH
+        )
+
     def iteration(it, carry):
-        more = it < ITERS - 1
         n = 2 * it + 2
-
-        @pl.when(more)
-        def _():
-            start_halo(n, S.at[0])
-            finish_halo(n, S.at[0])
-            sweep(n, S.at[0], S.at[1])
-            start_halo(n + 1, S.at[1])
+        pack(S.at[0])
+        start_halo(n, S.at[0])
+        finish_halo(n, S.at[0])
+        sweep(n, S.at[0], S.at[1])
+        pack(S.at[1])
+        start_halo(n + 1, S.at[1])
 
         @pl.when(is_solver)
         def _():
-            heard_from_faces(it)
-            FR[...] = pick(FP[...].astype(BF16), RF[it])
-            solve()
-            facing = lax.dot_general(XV[...], interp[...], NT, precision=HIGHEST, preferred_element_type=F32)
-            SD[...] = pick(FPT[...].astype(BF16), facing)
-            send_to_faces(it)
-
-        @pl.when(more)
-        def _():
-            finish_halo(n + 1, S.at[1])
-            sweep(n + 1, S.at[1], S.at[0])
-            wall_base()
-
-        relay = pltpu.make_async_remote_copy(
-            WN.at[it], WN.at[it], rsend.at[it], rrecv.at[it], device_id=other_core, device_id_type=MESH
-        )
+            answer(it)
+
+        finish_halo(n + 1, S.at[1])
+        sweep(n + 1, S.at[1], S.at[0])
+        wall_base()
+        beside_wall = relay(it, WN.at[it])
 
         @pl.when(on_wall)
         def _():
-            sent_to_solvers(it)
-            whole = RD.at[it]
-            pltpu.make_async_copy(whole, whole, drecv.at[it]).wait()
-            WN[it, 1, inner] = pick(AT[...].astype(BF16), RD[it])
-
-            @pl.when(more)
-            def _():
-                copies = wall_copies(it)
-                each(copies, lambda pair: pair[0].start())
-                each(copies, lambda pair: pair[1].wait_recv())
-                spread(it)
-                SF[...] = pick(AM[...].astype(BF16), PB[...] + wall_response(it))
-                send_to_solvers(it + 1, SF)
-                each(copies, lambda pair: pair[0].wait_send())
-
-            relay.start()
+            hear_wall(it)
+            copies = wall_copies(it)
+            each(copies, lambda pair: pair[0].start())
+            each(copies, lambda pair: pair[1].wait_recv())
+            spread(it)
+            SF[...] = pick(AM[...].astype(BF16), PB[...] + wall_response(it))
+            send_to_solvers(it + 1, SF)
+            beside_wall.start()
+            each(copies, lambda pair: pair[0].wait_send())
 
         @pl.when(off_wall)
         def _():
-            relay.wait_recv()
-
-        @pl.when(more)
-        def _():
-            @pl.when(off_wall)
-            def _():
-                spread(it)
-
-            update()
+            beside_wall.wait_recv()
+            spread(it)
+
+        update()
 
         @pl.when(on_wall)
         def _():
-            relay.wait_send()
+            beside_wall.wait_send()
 
         @pl.when(is_solver)
         def _():
@@ -605,18 +601,9 @@
 
         return carry
 
-    lax.fori_loop(0, ITERS, iteration, 0)
-
-    wall = WN[ITERS - 1, 1, inner]
-
-    def add(z, carry):
-        share, _ = profile(z + 1)
-        raised = share * wall
-        for c in range(NV):
-            S[0, c, z + 1] += source[c] * raised
-        return carry
-
-    lax.fori_loop(0, NZL, add, 0)
+    lax.fori_loop(0, ITERS - 1, iteration, 0)
+
+    last = ITERS - 1
     out = pltpu.make_async_copy(S.at[0, :, pl.ds(1, NZL)], state_out, load_sem.at[0])
     out.start()
 
@@ -627,19 +614,43 @@
 
     @pl.when(is_solver)
     def _():
+        answer(last)
         back = lax.dot_general(placed, XV[...], (((0,), (0,)), ((), ())), precision=HIGHEST, preferred_element_type=F32)
         DV[...] = back[:EBD]
         for t in range(1, NFY):
             disp_copy(t).start()
-        DR[...] = back[:EBD]
+        disp_out[...] = back[:EBD]
+
+    beside_wall = relay(last, WN.at[last, 1, pl.ds(PAD, CX)])
+
+    @pl.when(on_wall)
+    def _():
+        hear_wall(last)
+        beside_wall.start()
+
+    @pl.when(off_wall)
+    def _():
+        beside_wall.wait_recv()
+
+    for z in range(NZL):
+        share, _ = profile(z + 1)
+        raised_out[z] = share * WN[last, 1, inner]
+
+    @pl.when(on_wall)
+    def _():
+        beside_wall.wait_send()
+
+    @pl.when(is_solver)
+    def _():
+        sent_to_faces(last)
         for t in range(1, NFY):
             disp_copy(t).wait_send()
 
     @pl.when(not_solver)
     def _():
         disp_copy(1).wait_recv()
-
-    disp_out[...] = DR[...]
+        disp_out[...] = DR[...]
+
     out.wait()
 
 
@@ -650,14 +661,15 @@
     vmem = pl.BlockSpec(memory_space=pltpu.VMEM)
     dma = pltpu.SemaphoreType.DMA
     sweeps = 2 * ITERS
-    return pl.pallas_call(
+    before, raised, displacement = pl.pallas_call(
         kernel,
         out_shape=(
             jax.ShapeDtypeStruct(state.shape, F32),
+            jax.ShapeDtypeStruct(kappa.shape, F32),
             jax.ShapeDtypeStruct((EBD, EB), F32),
         ),
         in_specs=[hbm] * 11,
-        out_specs=(hbm, vmem),
+        out_specs=(hbm, vmem, vmem),
         scratch_shapes=[
             pltpu.SMEM((NV, NV), F32),
             pltpu.SMEM((NV,), F32),
@@ -713,12 +725,13 @@
             dma((ITERS,)),
         ],
         compiler_params=pltpu.CompilerParams(
-            collective_id=0, has_side_effects=True, vmem_limit_bytes=40 * 1024 * 1024
+            collective_id=0, has_side_effects=True, vmem_limit_bytes=60 * 1024 * 1024
         ),
     )(
         state, kappa, mix, press_weight, source_weight, interp, block_inverse, coupling, front_order,
         face_owner.reshape(1, -1), face_slot.reshape(1, -1),
     )
+    return before + source_weight[:, None, None, None] * raised[None], displacement
 
 
 def solution(mesh):

time: 102 us -> 95.7 us (0.938)
  local copies, waits for them, and re-layouts: 8.08 us -> 1.25 us
  other arithmetic: 0 us -> 2.1 us
  Pallas kernels: 92.7 us -> 91.6 us
    unnamed x24 -> x5, local copies, waits for them, and re-layouts: 8.08 us -> 1.25 us
    add x0 -> x1, other arithmetic: none -> 2.1 us  [on_device(): before + source_weight[:, None, None, None] * raised[None]]
    pallas_call x1, Pallas kernels: 92.7 us -> 91.6 us  [on_device(): pl.pallas_call(kernel, out_shape=(jax.ShapeDtypeStruct(state.shape, F32),...]
where the time goes in v3:
time: 95.7 us; the launch traced here: 95.6 us
  Pallas kernels  91.6 us (96%)
  other arithmetic  2.1 us (2%)
  local copies, waits for them, and re-layouts  1.25 us (1%)
    pallas_call x1, Pallas kernels, on_device(): pl.pallas_call(kernel, out_shape=(jax.ShapeDtypeStruct(state.shape, F32),...  91.6 us
    add x1, other arithmetic, on_device(): before + source_weight[:, None, None, None] * raised[None]  2.1 us

profile of v3, /device:TPU:1, one launch (start us, length us, event | category | flops | bytes accessed | tf_op | source)
XLA Modules:
  0.0 95.6 jit_solution(8595091577405204443)
XLA Ops:
  0.6 91.6 %shard_map.122 = (f32[5,8,32,128]{3,2,1,0:T(8,128)}, f32[8,32,128]{2,1,0:T(8,128)}, f32[16,128]{1,0:T(8,128)}) custom-call(f32[5,8,32,128]{3,2,1,0:T(8,128)} %state_in.1, f32[8,32,128]{2,1,0:T(8,128)} %kappa_in.1, f32[5,5]{1,0:T(8,128)} %mix_in.1, f32[5]{0:T(128)} %press_in.1, f32[5]{0:T(128)} %source_in.1, f32[128,128]{1,0:T(8,128)} %interp_in.1, ...), custom_call_target="tpu_custom_call" | custom-call | tf_op jit(solution)/shard_map/pallas_call | solution.py:664
  92.2 0.0 copy-start.1
  92.2 0.6 copy-done.1
  92.9 0.0 copy-start
  92.9 2.1 %multiply_add_fusion = f32[5,8,32,128]{3,2,1,0:T(8,128)} fusion(f32[5,8,32,128]{3,2,1,0:T(8,128)} %get-tuple-element.5, f32[8,32,128]{2,1,0:T(8,128)} %get-tuple-element.6, f32[5]{0:T(128)S(1)} %copy-done.1), kind=kLoop, calls=%fused_computation | loop fusion | flops 327680 | bytes 1441812 | tf_op jit(solution)/shard_map/add | solution.py:734
  95.0 0.0 copy-done
  95.0 0.6 copy.14
Async XLA Ops:
  92.2 0.7 copy-start.1
  92.9 2.1 %copy-start = (f32[16,128]{1,0:T(8,128)S(1)}, f32[16,128]{1,0:T(8,128)}, u32[]{:S(2)}) copy-start(f32[16,128]{1,0:T(8,128)} %get-tuple-element.11) | copy-start | bytes 24580

commit v4 on v3

--- a/solution.py
+++ b/solution.py
@@ -22,6 +22,7 @@
 CXE = CX + 2 * PAD
 NT = (((1,), (1,)), ((), ()))
 FAR_Y = (2, 1, 3, 0)
+AROUND = 11
 
 
 def far_first(step, ring):
@@ -42,9 +43,9 @@
     state_in, kappa_in, mix_in, press_in, source_in, interp_in, inverse_in, coupling_in, order_in, owner_in, slot_in,
     state_out, raised_out, disp_out,
     mix, press_weight, source_weight, interp, order, owner, slot,
-    S, K, KX, KE, BI, CO, R, XS, XR, YS, YR, YK, ZR, KZ, SL, SF, RF, SD, RD, FP, FPT, AM, AT, FR, XV, DV, DR,
-    WN, LP, LE, QB, PB,
-    load_sem, hsend, hrecv, fsend, frecv, dsend, drecv, osend, orecv, wsend, wrecv, rsend, rrecv,
+    S, K, KX, KE, BI, CO, R, XS, XR, YS, YR, YK, ZR, KZ, SL, SF, CS, RF, RC, SD, RD, FP, FPT, AM, AT, FR, XV, DV, DR,
+    WN, LP, LE, QB, PB, G, GW, IN, XO, XA,
+    load_sem, hsend, hrecv, fsend, frecv, dsend, drecv, osend, orecv, wsend, wrecv, rsend, rrecv, csend, crecv, xsend, xrecv,
 ):
     ix, iy, iz = lax.axis_index("fx"), lax.axis_index("fy"), lax.axis_index("fz")
     ring_z, ring_y = ix // RING_Y, ix % RING_Y
@@ -118,6 +119,16 @@
         def _():
             signal(barrier, (ix, iy, 0))
 
+        def greet_solvers(step, carry):
+            base = row_base(step)
+            for dy in FAR_Y:
+                signal(barrier, (base + turned_y[dy], turned_y[dy], iz))
+            return carry
+
+        lax.fori_loop(0, RING_Z - 1, greet_solvers, 0)
+        for dy in FAR_Y[:3]:
+            signal(barrier, (ring_z * RING_Y + turned_y[dy], turned_y[dy], iz))
+
     @pl.when(on_wall)
     def _():
         cores = {dy: (iy + turned_y[dy]) % 2 for dy in FAR_Y}
@@ -146,7 +157,7 @@
     signal(barrier, other_core)
     solver_count = is_solver.astype(jnp.int32)
     wall_count = on_wall.astype(jnp.int32)
-    expected = 1 + wall_count * (2 * NFX - solver_count) + solver_count * (2 * NFX - wall_count + NFY - 1)
+    expected = 1 + wall_count * (2 * NFX - solver_count) + solver_count * (2 * NFX - wall_count + NFY - 1 + NFX - 1)
     for present, device in sides + corners:
         expected = expected + present.astype(jnp.int32)
 
@@ -173,6 +184,8 @@
     AT[...] = lax.dot_general(unit, chosen, NT, preferred_element_type=F32)
     slot_rows = jnp.sum(chosen * (slot[...] + 1).astype(F32), axis=1, keepdims=True)
     SL[...] = jnp.broadcast_to(slot_rows, (CAP * NFX, CY))
+    target_of = jnp.sum(unit * (EBD * owner[...] + slot[...] + 1).astype(F32), axis=1, keepdims=True)
+    WN[ITERS, 1, PAD : PAD + CX] = jnp.broadcast_to(target_of, (CX, CY))
     block_rows = lax.broadcasted_iota(jnp.int32, (EBD, EB), 0)
     block_lanes = lax.broadcasted_iota(jnp.int32, (EBD, EB), 1)
     placed = jnp.zeros((EBD, EB), F32)
@@ -279,13 +292,10 @@
         KX.at[edge], KZ, osend.at[0], orecv.at[0], device_id=other_core, device_id_type=MESH
     )
 
-    def send_to_solvers(turn, rows_out):
-        target = RF.at[turn, pl.ds(CAP * (ix * NFY + iy), CAP)]
-
+    def send_to_solvers(rows_of, target, sent, heard):
         def send(to, y, core):
             pltpu.make_async_remote_copy(
-                rows_out.at[pl.ds(CAP * to, CAP)], target, fsend.at[turn], frecv.at[turn],
-                device_id=(to, y, core), device_id_type=MESH,
+                rows_of(to), target, sent, heard, device_id=(to, y, core), device_id_type=MESH
             ).start()
 
         def group(step, carry):
@@ -309,7 +319,21 @@
 
             @pl.when(is_solver)
             def _():
-                pltpu.make_async_copy(rows_out.at[pl.ds(CAP * ix, CAP)], target, frecv.at[turn]).start()
+                pltpu.make_async_copy(rows_of(ix), target, heard).start()
+
+    own_rows = pl.ds(CAP * (ix * NFY + iy), CAP)
+
+    def send_rows(turn, rows_out):
+        send_to_solvers(
+            lambda to: rows_out.at[pl.ds(CAP * to, CAP)], RF.at[turn, own_rows], fsend.at[turn], frecv.at[turn]
+        )
+
+    def send_pressure(turn):
+        @pl.when(on_wall)
+        def _():
+            SF[...] = pick(AM[...].astype(BF16), PB[...])
+
+        send_rows(turn, SF)
 
     def sent_to_solvers(turn):
         @pl.when(on_wall)
@@ -397,7 +421,7 @@
     pl.semaphore_wait(barrier, expected)
     start_halo(0, S.at[0])
     kappa_plane.start()
-    send_to_solvers(ITERS, SL)
+    send_rows(ITERS, SL)
     finish_halo(0, S.at[0])
     sweep(0, S.at[0], S.at[1])
     pack(S.at[1])
@@ -432,11 +456,7 @@
     wall_base()
     sent_to_solvers(ITERS)
 
-    @pl.when(on_wall)
-    def _():
-        SF[...] = pick(AM[...].astype(BF16), PB[...])
-
-    send_to_solvers(0, SF)
+    send_pressure(0)
 
     @pl.when(is_solver)
     def _():
@@ -504,13 +524,6 @@
 
     first_jump = (NZ - 1.0) / NZ - 2.0
 
-    def wall_response(it):
-        wide = KX[1] * (LP[0] + first_jump * LP[1])
-        edges = KE[0] * (LE[0] + first_jump * LE[1])
-        above = KX[2, inner] * ((NZ - 1.0) / NZ * LP[0, inner])
-        bend = ring_sum(wide, edges, 0.0, above, KX[1, inner])
-        return press_twice * LP[1, inner] + 2.0 * press_once * wide[inner] + press_source * bend
-
     def profile(plane):
         height = iz * NZL + plane - 1
         return 1.0 - height.astype(F32) / NZ, jnp.where(height == 0, first_jump, 0.0)
@@ -535,16 +548,128 @@
 
         lax.fori_loop(0, NZL, second, 0)
 
+    def tell_faces():
+        targets = (
+            [pltpu.roll(WN[ITERS, 1], (CXE - d) % CXE, 0)[inner] for d in range(-2, 3)]
+            + [pltpu.roll(WN[ITERS, 0], (CXE - d) % CXE, 0)[inner] for d in range(-1, 2)]
+            + [pltpu.roll(WN[ITERS, 2], (CXE - d) % CXE, 0)[inner] for d in range(-1, 2)]
+        )
+        facts = targets + [
+            jnp.broadcast_to(KE[0, :, CY - 1 : CY], (CX, CY)), jnp.broadcast_to(KE[0, :, 0:1], (CX, CY)),
+        ]
+        table = jnp.zeros((CX, CY), F32)
+        for n, fact in enumerate(facts):
+            table = jnp.where(lane == n, fact, table)
+        wall_coeff = KX[1]
+        selector = AM[...].astype(BF16)
+        CS[0] = pick(selector, table)
+        for n, d in enumerate((-1, 0, 1)):
+            CS[n + 1] = pick(selector, pltpu.roll(wall_coeff, (CXE - d) % CXE, 0)[inner])
+        CS[4] = pick(selector, KX[2, inner])
+
+    def send_facts():
+        send_to_solvers(lambda to: CS.at[:, pl.ds(CAP * to, CAP)], RC.at[:, own_rows], csend, crecv)
+
+    def sent_facts():
+        @pl.when(on_wall)
+        def _():
+            @pl.when(is_solver)
+            def _():
+                rest = RC.at[:, pl.ds(0, CAP * (2 * NFX - 1))]
+                pltpu.make_async_copy(rest, rest, csend).wait()
+
+            @pl.when(not_solver)
+            def _():
+                rest = RC.at[:, pl.ds(0, CAP * 2 * NFX)]
+                pltpu.make_async_copy(rest, rest, csend).wait()
+
+    def hear_facts():
+        pltpu.make_async_copy(RC, RC, crecv).wait()
+        names = lax.broadcasted_iota(jnp.int32, (FACES, NFX * EBD), 1) + 1
+        names = names.astype(F32)
+        for m in range(AROUND):
+            G[m] = jnp.where(names == RC[0, :, m : m + 1], 1.0, 0.0).astype(BF16)
+
+    def tell_solvers(it, facing):
+        if it:
+            rest = XA.at[0, pl.ds(0, (NFX - 1) * EBD)]
+            pltpu.make_async_copy(rest, rest, xsend.at[it - 1]).wait()
+        own = pick(placed.T[:EBD].astype(BF16), facing)
+        XO[...] = own
+        XA[it, pl.ds(EBD * ix, EBD)] = own
+
+        def send(to, y):
+            pltpu.make_async_remote_copy(
+                XO, XA.at[it, pl.ds(EBD * ix, EBD)], xsend.at[it], xrecv.at[it],
+                device_id=(to, y, iz), device_id_type=MESH,
+            ).start()
+
+        def group(step, carry):
+            base = row_base(step)
+            for dy in FAR_Y:
+                send(base + turned_y[dy], turned_y[dy])
+            return carry
+
+        lax.fori_loop(0, RING_Z - 1, group, 0)
+        for dy in FAR_Y[:3]:
+            send(ring_z * RING_Y + turned_y[dy], turned_y[dy])
+
+    def respond(it):
+        rest = XA.at[it, pl.ds(0, (NFX - 1) * EBD)]
+        pltpu.make_async_copy(rest, rest, xrecv.at[it]).wait()
+        high, low = split(XA[it])
+        both = jnp.concatenate([high, low], axis=1)
+        for m in range(AROUND):
+            found = jnp.dot(G[m], both, preferred_element_type=F32)
+            GW[m] = found[:, :CY] + found[:, CY:]
+
+        def chunk(n, carry):
+            at = pl.ds(pl.multiple_of(n * CX, CX), CX)
+            centre = {d: GW[d + 2, at] for d in range(-2, 3)}
+            beyond = {d: jnp.where(lane >= CY // 2, GW[d + 6, at], GW[d + 9, at]) for d in range(-1, 2)}
+            coeff = {d: RC[d + 2, at] for d in range(-1, 2)}
+
+            def wide_sum(d):
+                total = centre[d - 1] + centre[d + 1] - 4.0 * centre[d]
+                total += jnp.where(lane == 0, pltpu.roll(beyond[d], 1, 1), pltpu.roll(centre[d], 1, 1))
+                return total + jnp.where(
+                    lane == CY - 1, pltpu.roll(beyond[d], CY - 1, 1), pltpu.roll(centre[d], CY - 1, 1)
+                )
+
+            sums = {d: wide_sum(d) for d in range(-1, 2)}
+            slopes = {d: coeff[d] * (sums[d] + first_jump * centre[d]) for d in range(-1, 2)}
+            above = RC[4, at] * ((NZ - 1.0) / NZ * sums[0])
+            facts = RC[0, at]
+            edge_coeff = jnp.where(lane >= CY // 2, facts[:, AROUND : AROUND + 1], facts[:, AROUND + 1 : AROUND + 2])
+            edge_sum = beyond[-1] + beyond[1] - 4.0 * beyond[0]
+            edge_sum += jnp.where(
+                lane >= CY // 2,
+                pltpu.roll(beyond[0], 1, 1) + pltpu.roll(centre[0], CY - 1, 1),
+                pltpu.roll(beyond[0], CY - 1, 1) + pltpu.roll(centre[0], 1, 1),
+            )
+            edges = edge_coeff * (edge_sum + first_jump * beyond[0])
+            bend = slopes[-1] + slopes[1] + above - 6.0 * slopes[0]
+            bend += jnp.where(lane == 0, pltpu.roll(edges, 1, 1), pltpu.roll(slopes[0], 1, 1))
+            bend += jnp.where(lane == CY - 1, pltpu.roll(edges, CY - 1, 1), pltpu.roll(slopes[0], CY - 1, 1))
+            IN[at] = press_twice * centre[0] + 2.0 * press_once * slopes[0] + press_source * coeff[0] * bend
+            return carry
+
+        lax.fori_loop(0, FACES // CX, chunk, 0)
+
     def answer(it):
         heard_from_faces(it)
-        FR[...] = pick(FP[...].astype(BF16), RF[it])
+        if it:
+            sent_to_faces(it - 1)
+        rows_in = RF[it] + IN[...] if it else RF[it]
+        FR[...] = pick(FP[...].astype(BF16), rows_in)
         solve()
         facing = lax.dot_general(XV[...], interp[...], NT, precision=HIGHEST, preferred_element_type=F32)
+        if it < ITERS - 1:
+            tell_solvers(it, facing)
         SD[...] = pick(FPT[...].astype(BF16), facing)
         send_to_faces(it)
 
     def hear_wall(it):
-        sent_to_solvers(it)
         whole = RD.at[it]
         pltpu.make_async_copy(whole, whole, drecv.at[it]).wait()
         WN[it, 1, inner] = pick(AT[...].astype(BF16), RD[it])
@@ -554,54 +679,83 @@
             part, part, rsend.at[it], rrecv.at[it], device_id=other_core, device_id_type=MESH
         )
 
-    def iteration(it, carry):
+    around_wall = wall_copies(ITERS)
+
+    @pl.when(on_wall)
+    def _():
+        each(around_wall, lambda pair: pair[0].start())
+
+    for it in range(ITERS - 1):
         n = 2 * it + 2
         pack(S.at[0])
         start_halo(n, S.at[0])
+        if it == 0:
+
+            @pl.when(on_wall)
+            def _():
+                each(around_wall, lambda pair: pair[1].wait_recv())
+                tell_faces()
+                each(around_wall, lambda pair: pair[0].wait_send())
+
+            send_facts()
+        else:
+
+            @pl.when(is_solver)
+            def _():
+                answer(it)
+
         finish_halo(n, S.at[0])
         sweep(n, S.at[0], S.at[1])
         pack(S.at[1])
         start_halo(n + 1, S.at[1])
-
-        @pl.when(is_solver)
-        def _():
-            answer(it)
+        if it == 0:
+
+            @pl.when(is_solver)
+            def _():
+                answer(it)
 
         finish_halo(n + 1, S.at[1])
         sweep(n + 1, S.at[1], S.at[0])
         wall_base()
+        sent_to_solvers(it)
+        send_pressure(it + 1)
+        if it == 0:
+
+            @pl.when(is_solver)
+            def _():
+                hear_facts()
+
+        copies = wall_copies(it)
+
+        @pl.when(on_wall)
+        def _():
+            hear_wall(it)
+            each(copies, lambda pair: pair[0].start())
+
+        @pl.when(is_solver)
+        def _():
+            respond(it)
+
         beside_wall = relay(it, WN.at[it])
 
         @pl.when(on_wall)
         def _():
-            hear_wall(it)
-            copies = wall_copies(it)
-            each(copies, lambda pair: pair[0].start())
             each(copies, lambda pair: pair[1].wait_recv())
-            spread(it)
-            SF[...] = pick(AM[...].astype(BF16), PB[...] + wall_response(it))
-            send_to_solvers(it + 1, SF)
             beside_wall.start()
+
+        @pl.when(off_wall)
+        def _():
+            beside_wall.wait_recv()
+
+        spread(it)
+        update()
+
+        @pl.when(on_wall)
+        def _():
             each(copies, lambda pair: pair[0].wait_send())
-
-        @pl.when(off_wall)
-        def _():
-            beside_wall.wait_recv()
-            spread(it)
-
-        update()
-
-        @pl.when(on_wall)
-        def _():
             beside_wall.wait_send()
 
-        @pl.when(is_solver)
-        def _():
-            sent_to_faces(it)
-
-        return carry
-
-    lax.fori_loop(0, ITERS - 1, iteration, 0)
+    sent_facts()
 
     last = ITERS - 1
     out = pltpu.make_async_copy(S.at[0, :, pl.ds(1, NZL)], state_out, load_sem.at[0])
@@ -625,6 +779,7 @@
 
     @pl.when(on_wall)
     def _():
+        sent_to_solvers(last)
         hear_wall(last)
         beside_wall.start()
 
@@ -643,6 +798,8 @@
     @pl.when(is_solver)
     def _():
         sent_to_faces(last)
+        rest = XA.at[0, pl.ds(0, (NFX - 1) * EBD)]
+        pltpu.make_async_copy(rest, rest, xsend.at[last - 1]).wait()
         for t in range(1, NFY):
             disp_copy(t).wait_send()
 
@@ -694,7 +851,9 @@
             pltpu.VMEM((CXE, CY), F32),
             pltpu.VMEM((CAP * NFX, CY), F32),
             pltpu.VMEM((CAP * NFX, CY), F32),
+            pltpu.VMEM((5, CAP * NFX, CY), F32),
             pltpu.VMEM((ITERS + 1, FACES, CY), F32),
+            pltpu.VMEM((5, FACES, CY), F32),
             pltpu.VMEM((FACES, CY), F32),
             pltpu.VMEM((ITERS, CAP * NFX, CY), F32),
             pltpu.VMEM((EBD, FACES), F32),
@@ -705,11 +864,16 @@
             pltpu.VMEM((EBD, EB), F32),
             pltpu.VMEM((EBD, EB), F32),
             pltpu.VMEM((EBD, EB), F32),
-            pltpu.VMEM((ITERS, 3, CXE, CY), F32),
+            pltpu.VMEM((ITERS + 1, 3, CXE, CY), F32),
             pltpu.VMEM((2, CXE, CY), F32),
             pltpu.VMEM((2, CX, CY), F32),
             pltpu.VMEM((NZL + 2, CXE, CY), F32),
             pltpu.VMEM((CX, CY), F32),
+            pltpu.VMEM((AROUND, FACES, NFX * EBD), BF16),
+            pltpu.VMEM((AROUND, FACES, CY), F32),
+            pltpu.VMEM((FACES, CY), F32),
+            pltpu.VMEM((EBD, EB), F32),
+            pltpu.VMEM((ITERS - 1, NFX * EBD, EB), F32),
             dma((11,)),
             dma((sweeps, 5)),
             dma((sweeps, 5)),
@@ -719,10 +883,14 @@
             dma((ITERS,)),
             dma((NFY,)),
             dma((2,)),
-            dma((ITERS, 8)),
-            dma((ITERS, 8)),
+            dma((ITERS + 1, 8)),
+            dma((ITERS + 1, 8)),
             dma((ITERS,)),
             dma((ITERS,)),
+            dma,
+            dma,
+            dma((ITERS - 1,)),
+            dma((ITERS - 1,)),
         ],
         compiler_params=pltpu.CompilerParams(
             collective_id=0, has_side_effects=True, vmem_limit_bytes=60 * 1024 * 1024

time: 95.7 us -> 95.1 us (level)
  no operation moved by 1% of the time
where the time goes in v4:
time: 95.1 us; the launch traced here: 94.9 us
  Pallas kernels  90.9 us (96%)
  other arithmetic  2.1 us (2%)
  local copies, waits for them, and re-layouts  1.25 us (1%)
    pallas_call x1, Pallas kernels, on_device(): pl.pallas_call(kernel, out_shape=(jax.ShapeDtypeStruct(state.shape, F32),...  90.9 us
    add x1, other arithmetic, on_device(): before + source_weight[:, None, None, None] * raised[None]  2.1 us

profile of v4, /device:TPU:1, one launch (start us, length us, event | category | flops | bytes accessed | tf_op | source)
XLA Modules:
  0.0 94.9 jit_solution(7892391893803012359)
XLA Ops:
  0.6 90.9 %shard_map.122 = (f32[5,8,32,128]{3,2,1,0:T(8,128)}, f32[8,32,128]{2,1,0:T(8,128)}, f32[16,128]{1,0:T(8,128)}) custom-call(f32[5,8,32,128]{3,2,1,0:T(8,128)} %state_in.1, f32[8,32,128]{2,1,0:T(8,128)} %kappa_in.1, f32[5,5]{1,0:T(8,128)} %mix_in.1, f32[5]{0:T(128)} %press_in.1, f32[5]{0:T(128)} %source_in.1, f32[128,128]{1,0:T(8,128)} %interp_in.1, ...), custom_call_target="tpu_custom_call" | custom-call | tf_op jit(solution)/shard_map/pallas_call | solution.py:821
  91.6 0.0 copy-start.1
  91.6 0.6 copy-done.1
  92.2 0.0 copy-start
  92.2 2.1 %multiply_add_fusion = f32[5,8,32,128]{3,2,1,0:T(8,128)} fusion(f32[5,8,32,128]{3,2,1,0:T(8,128)} %get-tuple-element.5, f32[8,32,128]{2,1,0:T(8,128)} %get-tuple-element.6, f32[5]{0:T(128)S(1)} %copy-done.1), kind=kLoop, calls=%fused_computation | loop fusion | flops 327680 | bytes 1441812 | tf_op jit(solution)/shard_map/add | solution.py:902
  94.3 0.0 copy-done
  94.3 0.6 copy.14
Async XLA Ops:
  91.6 0.7 copy-start.1
  92.2 2.1 %copy-start = (f32[16,128]{1,0:T(8,128)S(1)}, f32[16,128]{1,0:T(8,128)}, u32[]{:S(2)}) copy-start(f32[16,128]{1,0:T(8,128)} %get-tuple-element.11) | copy-start | bytes 24580

commit v5 on v4

--- a/solution.py
+++ b/solution.py
@@ -51,7 +51,8 @@
     ring_z, ring_y = ix // RING_Y, ix % RING_Y
     on_wall = iz == 0
     off_wall = iz == 1
-    is_solver = iy == ring_y
+    home = (ring_y + ring_z) % NFY
+    is_solver = iy == home
     not_solver = jnp.logical_not(is_solver)
     turned_y = {d: (ring_y + d) % RING_Y for d in FAR_Y}
     turned_x = {d: (iy + d) % NFY for d in FAR_Y}
@@ -59,6 +60,15 @@
 
     def row_base(step):
         return ((ring_z + far_first(step, RING_Z)) % RING_Z) * RING_Y
+
+    def homes(z):
+        return {d: (turned_y[d] + z) % NFY for d in FAR_Y}
+
+    def owners_at(step):
+        z = (ring_z + far_first(step, RING_Z)) % RING_Z
+        return [(z * RING_Y + turned_y[d], home_y) for d, home_y in homes(z).items()]
+
+    near_owners = [(ring_z * RING_Y + turned_y[d], home_y) for d, home_y in homes(ring_z).items()][:3]
 
     def signal(barrier, device):
         pl.semaphore_signal(barrier, inc=1, device_id=device, device_id_type=MESH)
@@ -120,36 +130,32 @@
             signal(barrier, (ix, iy, 0))
 
         def greet_solvers(step, carry):
-            base = row_base(step)
-            for dy in FAR_Y:
-                signal(barrier, (base + turned_y[dy], turned_y[dy], iz))
+            for to, home_y in owners_at(step):
+                signal(barrier, (to, home_y, iz))
             return carry
 
         lax.fori_loop(0, RING_Z - 1, greet_solvers, 0)
-        for dy in FAR_Y[:3]:
-            signal(barrier, (ring_z * RING_Y + turned_y[dy], turned_y[dy], iz))
+        for to, home_y in near_owners:
+            signal(barrier, (to, home_y, iz))
 
     @pl.when(on_wall)
     def _():
-        cores = {dy: (iy + turned_y[dy]) % 2 for dy in FAR_Y}
-
         def greet(step, carry):
-            base = row_base(step)
-            for dy in FAR_Y:
-                signal(barrier, (base + turned_y[dy], turned_y[dy], cores[dy]))
+            for to, home_y in owners_at(step):
+                signal(barrier, (to, home_y, (iy + home_y) % 2))
             return carry
 
         lax.fori_loop(0, RING_Z - 1, greet, 0)
-        for dy in FAR_Y[:3]:
-            signal(barrier, (ring_z * RING_Y + turned_y[dy], turned_y[dy], cores[dy]))
+        for to, home_y in near_owners:
+            signal(barrier, (to, home_y, (iy + home_y) % 2))
 
         @pl.when(not_solver)
         def _():
-            signal(barrier, (ix, ring_y, cores[0]))
+            signal(barrier, (ix, home, (iy + home) % 2))
 
     @pl.when(not_solver)
     def _():
-        signal(barrier, (ix, ring_y, iz))
+        signal(barrier, (ix, home, iz))
 
     for ref in (XR, YR, WN):
         ref[...] = jnp.zeros_like(ref)
@@ -299,23 +305,22 @@
             ).start()
 
         def group(step, carry):
-            base = row_base(step)
-            for dy in FAR_Y:
+            for to, home_y in owners_at(step):
                 for core in range(2):
-                    send(base + turned_y[dy], turned_y[dy], core)
+                    send(to, home_y, core)
             return carry
 
         @pl.when(on_wall)
         def _():
             lax.fori_loop(0, RING_Z - 1, group, 0)
-            for dy in FAR_Y[:3]:
+            for to, home_y in near_owners:
                 for core in range(2):
-                    send(ring_z * RING_Y + turned_y[dy], turned_y[dy], core)
-            send(ix, ring_y, 1)
+                    send(to, home_y, core)
+            send(ix, home, 1)
 
             @pl.when(not_solver)
             def _():
-                send(ix, ring_y, 0)
+                send(ix, home, 0)
 
             @pl.when(is_solver)
             def _():
@@ -605,14 +610,13 @@
             ).start()
 
         def group(step, carry):
-            base = row_base(step)
-            for dy in FAR_Y:
-                send(base + turned_y[dy], turned_y[dy])
+            for to, home_y in owners_at(step):
+                send(to, home_y)
             return carry
 
         lax.fori_loop(0, RING_Z - 1, group, 0)
-        for dy in FAR_Y[:3]:
-            send(ring_z * RING_Y + turned_y[dy], turned_y[dy])
+        for to, home_y in near_owners:
+            send(to, home_y)
 
     def respond(it):
         rest = XA.at[it, pl.ds(0, (NFX - 1) * EBD)]
@@ -664,10 +668,12 @@
         FR[...] = pick(FP[...].astype(BF16), rows_in)
         solve()
         facing = lax.dot_general(XV[...], interp[...], NT, precision=HIGHEST, preferred_element_type=F32)
-        if it < ITERS - 1:
+        if 0 < it < ITERS - 1:
             tell_solvers(it, facing)
         SD[...] = pick(FPT[...].astype(BF16), facing)
         send_to_faces(it)
+        if it == 0:
+            tell_solvers(it, facing)
 
     def hear_wall(it):
         whole = RD.at[it]

time: 95.1 us -> 89.4 us (0.940)
  Pallas kernels: 90.9 us -> 85.3 us
    pallas_call x1, Pallas kernels: 90.9 us -> 85.3 us  [on_device(): pl.pallas_call(kernel, out_shape=(jax.ShapeDtypeStruct(state.shape, F32),...]
where the time goes in v5:
time: 89.4 us; the launch traced here: 89.3 us
  Pallas kernels  85.3 us (95%)
  other arithmetic  2.1 us (2%)
  local copies, waits for them, and re-layouts  1.25 us (1%)
    pallas_call x1, Pallas kernels, on_device(): pl.pallas_call(kernel, out_shape=(jax.ShapeDtypeStruct(state.shape, F32),...  85.3 us
    add x1, other arithmetic, on_device(): before + source_weight[:, None, None, None] * raised[None]  2.1 us

profile of v5, /device:TPU:1, one launch (start us, length us, event | category | flops | bytes accessed | tf_op | source)
XLA Modules:
  0.0 89.3 jit_solution(16674260001123600377)
XLA Ops:
  0.6 85.3 %shard_map.122 = (f32[5,8,32,128]{3,2,1,0:T(8,128)}, f32[8,32,128]{2,1,0:T(8,128)}, f32[16,128]{1,0:T(8,128)}) custom-call(f32[5,8,32,128]{3,2,1,0:T(8,128)} %state_in.1, f32[8,32,128]{2,1,0:T(8,128)} %kappa_in.1, f32[5,5]{1,0:T(8,128)} %mix_in.1, f32[5]{0:T(128)} %press_in.1, f32[5]{0:T(128)} %source_in.1, f32[128,128]{1,0:T(8,128)} %interp_in.1, ...), custom_call_target="tpu_custom_call" | custom-call | tf_op jit(solution)/shard_map/pallas_call | solution.py:827
  85.9 0.0 copy-start.1
  85.9 0.6 copy-done.1
  86.6 0.0 copy-start
  86.6 2.1 %multiply_add_fusion = f32[5,8,32,128]{3,2,1,0:T(8,128)} fusion(f32[5,8,32,128]{3,2,1,0:T(8,128)} %get-tuple-element.5, f32[8,32,128]{2,1,0:T(8,128)} %get-tuple-element.6, f32[5]{0:T(128)S(1)} %copy-done.1), kind=kLoop, calls=%fused_computation | loop fusion | flops 327680 | bytes 1441812 | tf_op jit(solution)/shard_map/add | solution.py:908
  88.7 0.0 copy-done
  88.7 0.6 copy.14
Async XLA Ops:
  85.9 0.7 copy-start.1
  86.6 2.1 %copy-start = (f32[16,128]{1,0:T(8,128)S(1)}, f32[16,128]{1,0:T(8,128)}, u32[]{:S(2)}) copy-start(f32[16,128]{1,0:T(8,128)} %get-tuple-element.11) | copy-start | bytes 24580

commit v6 on v5

--- a/solution.py
+++ b/solution.py
@@ -203,31 +203,33 @@
     for load in loads[3:5]:
         load.wait()
 
-    def kappa_faces(z, carry):
-        low, high = carry
+    pair = lane // 2
+
+    def put_ends(ends, centre, at):
+        return jnp.where(pair == at, pltpu.roll(centre, 2 * at + 1, 1), ends)
+
+    def take_ends(n):
+        return jnp.where(lane % 2 == 0, pltpu.roll(YR[n, 1], CY - 1, 1), pltpu.roll(YR[n, 0], 1, 1))
+
+    def kappa_faces(z, ends):
         coeff = DIFFUSION * K[z]
         KX[z + 1, PAD : PAD + CX] = coeff
         XS[0, NV, pl.ds(z, 1), :] = coeff[0:1]
         XS[1, NV, pl.ds(z, 1), :] = coeff[CX - 1 : CX]
-        here = lane == NV * NZL + z
-        return jnp.where(here, coeff[:, 0:1], low), jnp.where(here, coeff[:, CY - 1 : CY], high)
-
-    nothing = jnp.zeros((CX, CY), F32)
-    YK[0], YK[1] = lax.fori_loop(0, NZL, kappa_faces, (nothing, nothing))
+        return put_ends(ends, coeff, NV * NZL + z)
+
+    YK[...] = lax.fori_loop(0, NZL, kappa_faces, jnp.zeros((CX, CY), F32))
 
     def pack(src):
-        def plane(z, carry):
-            low, high = carry
+        def plane(z, ends):
             for c in range(NV):
                 centre = src[c, z + 1]
                 XS[0, c, pl.ds(z, 1), :] = centre[0:1]
                 XS[1, c, pl.ds(z, 1), :] = centre[CX - 1 : CX]
-                here = lane == c * NZL + z
-                low = jnp.where(here, centre[:, 0:1], low)
-                high = jnp.where(here, centre[:, CY - 1 : CY], high)
-            return low, high
-
-        YS[0], YS[1] = lax.fori_loop(0, NZL, plane, (YK[0], YK[1]))
+                ends = put_ends(ends, centre, c * NZL + z)
+            return ends
+
+        YS[...] = lax.fori_loop(0, NZL, plane, YK[...])
 
     edge = NZL - (NZL - 1) * iz
 
@@ -243,15 +245,15 @@
         sends = (
             (has_left, remote(XS.at[0], XR.at[n, 1], 0, 1, left)),
             (has_right, remote(XS.at[1], XR.at[n, 0], 1, 0, right)),
-            (has_front, remote(YS.at[0], YR.at[n, 1], 2, 3, front)),
-            (has_back, remote(YS.at[1], YR.at[n, 0], 3, 2, back)),
+            (has_front, remote(YS, YR.at[n, 1], 2, 3, front)),
+            (has_back, remote(YS, YR.at[n, 0], 3, 2, back)),
             (always, remote(plane, ZR.at[n], 4, 4, other_core)),
         )
         waits = (
             (has_left, remote(XS.at[0], XR.at[n, 0], 0, 0, left)),
             (has_right, remote(XS.at[1], XR.at[n, 1], 1, 1, right)),
-            (has_front, remote(YS.at[0], YR.at[n, 0], 2, 2, front)),
-            (has_back, remote(YS.at[1], YR.at[n, 1], 3, 3, back)),
+            (has_front, remote(YS, YR.at[n, 0], 2, 2, front)),
+            (has_back, remote(YS, YR.at[n, 1], 3, 3, back)),
             (always, remote(plane, ZR.at[n], 4, 4, other_core)),
         )
         return sends, waits
@@ -267,12 +269,13 @@
         each(halo_copies(n, src)[0], lambda copy: copy.start())
 
     def finish_halo(n, src):
-        sends, waits = halo_copies(n, src)
+        _, waits = halo_copies(n, src)
         each(waits, lambda copy: copy.wait_recv())
-        each(sends, lambda copy: copy.wait_send())
         src[:, (NZL + 1) * (1 - iz)] = ZR[n]
 
     def sweep(n, src, dst):
+        outer = take_ends(n)
+
         def plane(z, carry):
             coeff = KX[z + 1, PAD : PAD + CX]
             centres = [src[c, z + 1] for c in range(NV)]
@@ -282,10 +285,9 @@
                 beside = src[c, z] + src[c, z + 2]
                 beside += jnp.where(row == 0, XR[n, 0, c, pl.ds(z, 1), :], pltpu.roll(centre, 1, 0))
                 beside += jnp.where(row == CX - 1, XR[n, 1, c, pl.ds(z, 1), :], pltpu.roll(centre, CX - 1, 0))
-                front = pltpu.roll(YR[n, 0], (CY - at) % CY, 1)
-                back = pltpu.roll(YR[n, 1], CY - 1 - at, 1)
-                beside += jnp.where(lane == 0, front, pltpu.roll(centre, 1, 1))
-                beside += jnp.where(lane == CY - 1, back, pltpu.roll(centre, CY - 1, 1))
+                ends = pltpu.roll(outer, CY - 1 - 2 * at, 1)
+                beside += jnp.where(lane == 0, ends, pltpu.roll(centre, 1, 1))
+                beside += jnp.where(lane == CY - 1, ends, pltpu.roll(centre, CY - 1, 1))
                 total = centre + coeff * (beside - 6.0 * centre)
                 for d in range(NV):
                     total += mix[c, d] * centres[d]
@@ -293,6 +295,7 @@
             return carry
 
         lax.fori_loop(0, NZL, plane, 0)
+        each(halo_copies(n, src)[0], lambda copy: copy.wait_send())
 
     kappa_plane = pltpu.make_async_remote_copy(
         KX.at[edge], KZ, osend.at[0], orecv.at[0], device_id=other_core, device_id_type=MESH
@@ -437,12 +440,14 @@
     KX[(NZL + 1) * iz] = jnp.zeros((CXE, CY), F32)
     tile_row = lax.broadcasted_iota(jnp.int32, (PAD, CY), 0)
 
+    ends = take_ends(0)
+
     def kappa_edges(z, carry):
         KX[z + 1, 0:PAD] = jnp.where(tile_row == PAD - 1, XR[0, 0, NV, pl.ds(z, 1), :], 0.0)
         KX[z + 1, PAD + CX : CXE] = jnp.where(tile_row == 0, XR[0, 1, NV, pl.ds(z, 1), :], 0.0)
-        at = NV * NZL + z
-        front = pltpu.roll(YR[0, 0], CY - 1 - at, 1)
-        back = pltpu.roll(YR[0, 1], (CY - at) % CY, 1)
+        at = 2 * (NV * NZL + z)
+        front = pltpu.roll(ends, CY - 2 - at, 1)
+        back = pltpu.roll(ends, CY - at, 1)
         KE[z] = jnp.where(lane >= CY // 2, front, back)
         return carry
 
@@ -815,6 +820,32 @@
         disp_out[...] = DR[...]
 
     out.wait()
+
+
+def last_add(before, raised, source_in, displacement, state_out, disp_out, T, A, D, source_weight, load_sem, out_sem):
+    weights = pltpu.make_async_copy(source_in, source_weight, load_sem.at[NV])
+    heights = pltpu.make_async_copy(raised, A, load_sem.at[NV + 1])
+    small_in = pltpu.make_async_copy(displacement, D, load_sem.at[NV + 2])
+    loads = [pltpu.make_async_copy(before.at[c], T.at[c], load_sem.at[c]) for c in range(NV)]
+    stores = [pltpu.make_async_copy(T.at[c], state_out.at[c], out_sem.at[c]) for c in range(NV)]
+    small_out = pltpu.make_async_copy(D, disp_out, out_sem.at[NV])
+    for copy in [weights, heights] + loads + [small_in]:
+        copy.start()
+    weights.wait()
+    heights.wait()
+    for c in range(NV):
+        loads[c].wait()
+
+        def plane(z, carry):
+            T[c, z] += source_weight[c] * A[z]
+            return carry
+
+        lax.fori_loop(0, NZL, plane, 0)
+        stores[c].start()
+    small_in.wait()
+    small_out.start()
+    for copy in stores + [small_out]:
+        copy.wait()
 
 
 def on_device(
@@ -850,9 +881,9 @@
             pltpu.VMEM((EBD, 2 * EB, 2 * EB), BF16),
             pltpu.VMEM((2, NV + 1, NZL, CY), F32),
             pltpu.VMEM((sweeps, 2, NV + 1, NZL, CY), F32),
-            pltpu.VMEM((2, CX, CY), F32),
+            pltpu.VMEM((CX, CY), F32),
             pltpu.VMEM((sweeps, 2, CX, CY), F32),
-            pltpu.VMEM((2, CX, CY), F32),
+            pltpu.VMEM((CX, CY), F32),
             pltpu.VMEM((sweeps, NV, CX, CY), F32),
             pltpu.VMEM((CXE, CY), F32),
             pltpu.VMEM((CAP * NFX, CY), F32),
@@ -905,7 +936,24 @@
         state, kappa, mix, press_weight, source_weight, interp, block_inverse, coupling, front_order,
         face_owner.reshape(1, -1), face_slot.reshape(1, -1),
     )
-    return before + source_weight[:, None, None, None] * raised[None], displacement
+    return pl.pallas_call(
+        last_add,
+        out_shape=(
+            jax.ShapeDtypeStruct(state.shape, F32),
+            jax.ShapeDtypeStruct((EBD, EB), F32),
+        ),
+        in_specs=[hbm] * 4,
+        out_specs=(hbm, hbm),
+        scratch_shapes=[
+            pltpu.VMEM((NV, NZL, CX, CY), F32),
+            pltpu.VMEM((NZL, CX, CY), F32),
+            pltpu.VMEM((EBD, EB), F32),
+            pltpu.SMEM((NV,), F32),
+            dma((NV + 3,)),
+            dma((NV + 1,)),
+        ],
+        compiler_params=pltpu.CompilerParams(vmem_limit_bytes=60 * 1024 * 1024),
+    )(before, raised, source_weight, displacement)
 
 
 def solution(mesh):

time: 89.4 us -> 87.6 us (0.980)
  other arithmetic: 2.1 us -> 0 us
  Pallas kernels: 85.3 us -> 86.8 us
  local copies, waits for them, and re-layouts: 1.25 us -> 0 us
    add x1 -> x0, other arithmetic: 2.1 us -> none  [on_device(): before + source_weight[:, None, None, None] * raised[None]]
    pallas_call x0 -> x1, Pallas kernels: none -> 2.06 us  [on_device(): pl.pallas_call(last_add, out_shape=(jax.ShapeDtypeStruct(state.shape, F32...]
    unnamed x5 -> x0, local copies, waits for them, and re-layouts: 1.25 us -> none
where the time goes in v6:
time: 87.6 us; the launch traced here: 87.5 us
  Pallas kernels  86.8 us (99%)
    pallas_call x1, Pallas kernels, on_device(): pl.pallas_call(kernel, out_shape=(jax.ShapeDtypeStruct(state.shape, F32),...  84.8 us
    pallas_call x1, Pallas kernels, on_device(): pl.pallas_call(last_add, out_shape=(jax.ShapeDtypeStruct(state.shape, F32...  2.06 us

profile of v6, /device:TPU:1, one launch (start us, length us, event | category | flops | bytes accessed | tf_op | source)
XLA Modules:
  0.0 87.5 jit_solution(13290340296323944026)
XLA Ops:
  0.6 84.8 %shard_map.122 = (f32[5,8,32,128]{3,2,1,0:T(8,128)}, f32[8,32,128]{2,1,0:T(8,128)}, f32[16,128]{1,0:T(8,128)}) custom-call(f32[5,8,32,128]{3,2,1,0:T(8,128)} %state_in.1, f32[8,32,128]{2,1,0:T(8,128)} %kappa_in.1, f32[5,5]{1,0:T(8,128)} %mix_in.1, f32[5]{0:T(128)} %press_in.1, f32[5]{0:T(128)} %source_in.3, f32[128,128]{1,0:T(8,128)} %interp_in.1, ...), custom_call_target="tpu_custom_call" | custom-call | tf_op jit(solution)/shard_map/pallas_call | solution.py:858
  85.4 2.1 %shard_map.123 = (f32[5,8,32,128]{3,2,1,0:T(8,128)}, f32[16,128]{1,0:T(8,128)}) custom-call(f32[5,8,32,128]{3,2,1,0:T(8,128)} %get-tuple-element.5.before, f32[8,32,128]{2,1,0:T(8,128)} %get-tuple-element.6.raised, f32[5]{0:T(128)} %source_in.3, f32[16,128]{1,0:T(8,128)} %get-tuple-element.7.displacement), custom_call_target="tpu_custom_call" | custom-call | tf_op jit(solution)/shard_map/pallas_call | solution.py:939

commit v7 on v6

--- a/solution.py
+++ b/solution.py
@@ -17,6 +17,7 @@
 NFX, NFY = 32, 4
 RING_Z, RING_Y = 8, 4
 EB, EBD, CAP = 128, 16, 2
+PAIRS = EBD // 2
 FACES = NFX * NFY * CAP
 PAD = 8
 CXE = CX + 2 * PAD
@@ -43,7 +44,7 @@
     state_in, kappa_in, mix_in, press_in, source_in, interp_in, inverse_in, coupling_in, order_in, owner_in, slot_in,
     state_out, raised_out, disp_out,
     mix, press_weight, source_weight, interp, order, owner, slot,
-    S, K, KX, KE, BI, CO, R, XS, XR, YS, YR, YK, ZR, KZ, SL, SF, CS, RF, RC, SD, RD, FP, FPT, AM, AT, FR, XV, DV, DR,
+    S, K, KX, KE, BI, CO, R, RO, RN, XS, XR, YS, YR, YK, ZR, KZ, SL, SF, CS, RF, RC, SD, RD, FP, FPT, AM, AT, FR, XV, DV, DR,
     WN, LP, LE, QB, PB, G, GW, IN, XO, XA,
     load_sem, hsend, hrecv, fsend, frecv, dsend, drecv, osend, orecv, wsend, wrecv, rsend, rrecv, csend, crecv, xsend, xrecv,
 ):
@@ -273,7 +274,7 @@
         each(waits, lambda copy: copy.wait_recv())
         src[:, (NZL + 1) * (1 - iz)] = ZR[n]
 
-    def sweep(n, src, dst):
+    def sweep(n, src, dst, first=0, end=NZL):
         outer = take_ends(n)
 
         def plane(z, carry):
@@ -294,8 +295,9 @@
                 dst[c, z + 1] = total
             return carry
 
-        lax.fori_loop(0, NZL, plane, 0)
-        each(halo_copies(n, src)[0], lambda copy: copy.wait_send())
+        lax.fori_loop(first, end, plane, 0)
+        if end == NZL:
+            each(halo_copies(n, src)[0], lambda copy: copy.wait_send())
 
     kappa_plane = pltpu.make_async_remote_copy(
         KX.at[edge], KZ, osend.at[0], orecv.at[0], device_id=other_core, device_id_type=MESH
@@ -406,16 +408,28 @@
 
     @pl.when(is_solver)
     def _():
-        def products(k, carry):
+        def parts(k):
             block = order[0, k]
             inverse = BI[block]
             force_part = lax.dot_general(interp[...], inverse, NT, precision=HIGHEST, preferred_element_type=F32)
             chain = jnp.dot(inverse, CO[block], precision=HIGHEST, preferred_element_type=F32)
-            high, low = split(jnp.concatenate([force_part, -chain.T], axis=0))
-            R[k] = jnp.concatenate([high, low], axis=1)
-            return carry
-
-        lax.fori_loop(0, EBD, products, 0)
+            return force_part, -chain.T
+
+        def both_parts(matrix):
+            high, low = split(matrix)
+            return jnp.concatenate([high, low], axis=1)
+
+        def products(m, carry):
+            force, chain = parts(2 * m)
+            next_force, next_chain = parts(2 * m + 1)
+            passed = jnp.dot(force, next_chain, precision=HIGHEST, preferred_element_type=F32)
+            leap = jnp.dot(chain, next_chain, precision=HIGHEST, preferred_element_type=F32)
+            R[m] = both_parts(jnp.concatenate([force, chain], axis=0))
+            RO[m] = both_parts(jnp.concatenate([next_force, passed], axis=0))
+            RN[m] = both_parts(leap)
+            return carry
+
+        lax.fori_loop(0, PAIRS, products, 0)
 
     numbers = range(NV)
     source = [source_weight[c] for c in numbers]
@@ -425,68 +439,7 @@
     press_once = sum(press_weight[c] * once[c] for c in numbers)
     press_twice = sum(press_weight[c] * twice[c] for c in numbers)
 
-    pack(S.at[0])
-    pl.semaphore_wait(barrier, expected)
-    start_halo(0, S.at[0])
-    kappa_plane.start()
-    send_rows(ITERS, SL)
-    finish_halo(0, S.at[0])
-    sweep(0, S.at[0], S.at[1])
-    pack(S.at[1])
-    start_halo(1, S.at[1])
-
-    kappa_plane.wait()
-    KX[(NZL + 1) * (1 - iz)] = KZ[...]
-    KX[(NZL + 1) * iz] = jnp.zeros((CXE, CY), F32)
-    tile_row = lax.broadcasted_iota(jnp.int32, (PAD, CY), 0)
-
-    ends = take_ends(0)
-
-    def kappa_edges(z, carry):
-        KX[z + 1, 0:PAD] = jnp.where(tile_row == PAD - 1, XR[0, 0, NV, pl.ds(z, 1), :], 0.0)
-        KX[z + 1, PAD + CX : CXE] = jnp.where(tile_row == 0, XR[0, 1, NV, pl.ds(z, 1), :], 0.0)
-        at = 2 * (NV * NZL + z)
-        front = pltpu.roll(ends, CY - 2 - at, 1)
-        back = pltpu.roll(ends, CY - at, 1)
-        KE[z] = jnp.where(lane >= CY // 2, front, back)
-        return carry
-
-    lax.fori_loop(0, NZL, kappa_edges, 0)
-
-    def wall_base():
-        @pl.when(on_wall)
-        def _():
-            pressure = press_weight[0] * S[0, 0, 1]
-            for c in range(1, NV):
-                pressure += press_weight[c] * S[0, c, 1]
-            PB[...] = pressure
-
-    finish_halo(1, S.at[1])
-    sweep(1, S.at[1], S.at[0])
-    wall_base()
-    sent_to_solvers(ITERS)
-
-    send_pressure(0)
-
-    @pl.when(is_solver)
-    def _():
-        heard_from_faces(ITERS)
-        face_lanes = lax.broadcasted_iota(jnp.int32, (FACES, EB), 1) + 1
-        slot_of = (RF[ITERS] == face_lanes.astype(F32)).astype(F32)
-        FP[...] = lax.dot_general(placed, slot_of, NT, preferred_element_type=F32)
-        FPT[...] = lax.dot_general(slot_of, placed, NT, preferred_element_type=F32)
-
-    def solve():
-        for k in range(EBD):
-            force = FR[pl.ds(k, 1), :]
-            previous = XV[pl.ds(k - 1, 1), :] if k else jnp.zeros((1, EB), F32)
-            both = jnp.concatenate([force, previous], axis=1)
-            high = both.astype(BF16).astype(F32)
-            at = lax.broadcasted_iota(jnp.int32, (8, 2 * EB), 0)
-            left = jnp.where(at == 0, high, jnp.where(at == 1, both - high, 0.0)).astype(BF16)
-            result = jnp.dot(left, R[k], preferred_element_type=F32)
-            summed = result[:, :EB] + result[:, EB:]
-            XV[pl.ds(k, 1), :] = summed[0:1] + summed[1:2]
+    inner = slice(PAD, PAD + CX)
 
     def wall_copies(it):
         def remote(n, opposite, source_row, side, target_row, count, device):
@@ -509,54 +462,6 @@
             (rf, remote(6, 5, high, 2, 0, 8, right_front)),
             (rb, remote(7, 4, high, 0, 0, 8, right_back)),
         )
-
-    lane_e = lax.broadcasted_iota(jnp.int32, (CXE, CY), 1)
-    inner = slice(PAD, PAD + CX)
-
-    def spread(it):
-        centre = WN[it, 1]
-        beyond = jnp.where(lane_e >= CY // 2, WN[it, 0], WN[it, 2])
-        up, down = pltpu.roll(centre, 1, 1), pltpu.roll(centre, CY - 1, 1)
-        out_up, out_down = pltpu.roll(beyond, 1, 1), pltpu.roll(beyond, CY - 1, 1)
-        lap = pltpu.roll(centre, 1, 0) + pltpu.roll(centre, CXE - 1, 0) - 4.0 * centre
-        lap += jnp.where(lane_e == 0, out_up, up) + jnp.where(lane_e == CY - 1, out_down, down)
-        lap_e = pltpu.roll(beyond, 1, 0) + pltpu.roll(beyond, CXE - 1, 0) - 4.0 * beyond
-        lap_e += jnp.where(lane_e >= CY // 2, out_up + down, out_down + up)
-        LP[0], LP[1] = lap, centre
-        LE[0], LE[1] = lap_e[inner], beyond[inner]
-
-    def ring_sum(wide, edge_columns, below, above, coeff):
-        own = wide[inner]
-        total = pltpu.roll(wide, 1, 0)[inner] + pltpu.roll(wide, CXE - 1, 0)[inner] + below + above - 6.0 * own
-        total += jnp.where(lane == 0, pltpu.roll(edge_columns, 1, 1), pltpu.roll(own, 1, 1))
-        total += jnp.where(lane == CY - 1, pltpu.roll(edge_columns, CY - 1, 1), pltpu.roll(own, CY - 1, 1))
-        return coeff * total
-
-    first_jump = (NZ - 1.0) / NZ - 2.0
-
-    def profile(plane):
-        height = iz * NZL + plane - 1
-        return 1.0 - height.astype(F32) / NZ, jnp.where(height == 0, first_jump, 0.0)
-
-    def update():
-        def first(plane, carry):
-            share, jump = profile(plane)
-            QB[plane] = KX[plane] * (share * LP[0] + jump * LP[1])
-            return carry
-
-        lax.fori_loop(0, NZL + 2, first, 0)
-
-        def second(z, carry):
-            share, jump = profile(z + 1)
-            edges = KE[z] * (share * LE[0] + jump * LE[1])
-            wide = QB[z + 1]
-            bend = ring_sum(wide, edges, QB[z, inner], QB[z + 2, inner], KX[z + 1, inner])
-            raised, slope = share * LP[1, inner], wide[inner]
-            for c in range(NV):
-                S[0, c, z + 1] += twice[c] * raised + 2.0 * once[c] * slope + source[c] * bend
-            return carry
-
-        lax.fori_loop(0, NZL, second, 0)
 
     def tell_faces():
         targets = (
@@ -580,6 +485,137 @@
     def send_facts():
         send_to_solvers(lambda to: CS.at[:, pl.ds(CAP * to, CAP)], RC.at[:, own_rows], csend, crecv)
 
+    around_wall = wall_copies(ITERS)
+    pack(S.at[0])
+    pl.semaphore_wait(barrier, expected)
+    start_halo(0, S.at[0])
+
+    @pl.when(on_wall)
+    def _():
+        each(around_wall, lambda pair: pair[0].start())
+
+    kappa_plane.start()
+    send_rows(ITERS, SL)
+    finish_halo(0, S.at[0])
+    sweep(0, S.at[0], S.at[1])
+    pack(S.at[1])
+    start_halo(1, S.at[1])
+
+    kappa_plane.wait()
+    KX[(NZL + 1) * (1 - iz)] = KZ[...]
+    KX[(NZL + 1) * iz] = jnp.zeros((CXE, CY), F32)
+    tile_row = lax.broadcasted_iota(jnp.int32, (PAD, CY), 0)
+
+    ends = take_ends(0)
+
+    def kappa_edges(z, carry):
+        KX[z + 1, 0:PAD] = jnp.where(tile_row == PAD - 1, XR[0, 0, NV, pl.ds(z, 1), :], 0.0)
+        KX[z + 1, PAD + CX : CXE] = jnp.where(tile_row == 0, XR[0, 1, NV, pl.ds(z, 1), :], 0.0)
+        at = 2 * (NV * NZL + z)
+        front = pltpu.roll(ends, CY - 2 - at, 1)
+        back = pltpu.roll(ends, CY - at, 1)
+        KE[z] = jnp.where(lane >= CY // 2, front, back)
+        return carry
+
+    lax.fori_loop(0, NZL, kappa_edges, 0)
+
+    @pl.when(on_wall)
+    def _():
+        each(around_wall, lambda pair: pair[1].wait_recv())
+        tell_faces()
+        each(around_wall, lambda pair: pair[0].wait_send())
+
+    send_facts()
+
+    def wall_base():
+        @pl.when(on_wall)
+        def _():
+            pressure = press_weight[0] * S[0, 0, 1]
+            for c in range(1, NV):
+                pressure += press_weight[c] * S[0, c, 1]
+            PB[...] = pressure
+
+    finish_halo(1, S.at[1])
+    sweep(1, S.at[1], S.at[0], 0, 1)
+    wall_base()
+    send_pressure(0)
+    sweep(1, S.at[1], S.at[0], 1, NZL)
+    sent_to_solvers(ITERS)
+
+    @pl.when(is_solver)
+    def _():
+        heard_from_faces(ITERS)
+        face_lanes = lax.broadcasted_iota(jnp.int32, (FACES, EB), 1) + 1
+        slot_of = (RF[ITERS] == face_lanes.astype(F32)).astype(F32)
+        FP[...] = lax.dot_general(placed, slot_of, NT, preferred_element_type=F32)
+        FPT[...] = lax.dot_general(slot_of, placed, NT, preferred_element_type=F32)
+
+    def times(row_in, matrix):
+        width = row_in.shape[1]
+        high = row_in.astype(BF16).astype(F32)
+        at = lax.broadcasted_iota(jnp.int32, (8, width), 0)
+        left = jnp.where(at == 0, high, jnp.where(at == 1, row_in - high, 0.0)).astype(BF16)
+        result = jnp.dot(left, matrix, preferred_element_type=F32)
+        summed = result[:, :EB] + result[:, EB:]
+        return summed[0:1] + summed[1:2]
+
+    def solve():
+        force = [FR[pl.ds(k, 1), :] for k in range(EBD)]
+        odd = [times(jnp.concatenate([force[2 * m + 1], force[2 * m]], axis=1), RO[m]) for m in range(PAIRS)]
+        for m in range(PAIRS):
+            if m:
+                odd[m] += times(odd[m - 1], RN[m])
+            XV[pl.ds(2 * m + 1, 1), :] = odd[m]
+            previous = odd[m - 1] if m else jnp.zeros((1, EB), F32)
+            XV[pl.ds(2 * m, 1), :] = times(jnp.concatenate([force[2 * m], previous], axis=1), R[m])
+
+    lane_e = lax.broadcasted_iota(jnp.int32, (CXE, CY), 1)
+
+    def spread(it):
+        centre = WN[it, 1]
+        beyond = jnp.where(lane_e >= CY // 2, WN[it, 0], WN[it, 2])
+        up, down = pltpu.roll(centre, 1, 1), pltpu.roll(centre, CY - 1, 1)
+        out_up, out_down = pltpu.roll(beyond, 1, 1), pltpu.roll(beyond, CY - 1, 1)
+        lap = pltpu.roll(centre, 1, 0) + pltpu.roll(centre, CXE - 1, 0) - 4.0 * centre
+        lap += jnp.where(lane_e == 0, out_up, up) + jnp.where(lane_e == CY - 1, out_down, down)
+        lap_e = pltpu.roll(beyond, 1, 0) + pltpu.roll(beyond, CXE - 1, 0) - 4.0 * beyond
+        lap_e += jnp.where(lane_e >= CY // 2, out_up + down, out_down + up)
+        LP[0], LP[1] = lap, centre
+        LE[0], LE[1] = lap_e[inner], beyond[inner]
+
+    def ring_sum(wide, edge_columns, below, above, coeff):
+        own = wide[inner]
+        total = pltpu.roll(wide, 1, 0)[inner] + pltpu.roll(wide, CXE - 1, 0)[inner] + below + above - 6.0 * own
+        total += jnp.where(lane == 0, pltpu.roll(edge_columns, 1, 1), pltpu.roll(own, 1, 1))
+        total += jnp.where(lane == CY - 1, pltpu.roll(edge_columns, CY - 1, 1), pltpu.roll(own, CY - 1, 1))
+        return coeff * total
+
+    first_jump = (NZ - 1.0) / NZ - 2.0
+
+    def profile(plane):
+        height = iz * NZL + plane - 1
+        return 1.0 - height.astype(F32) / NZ, jnp.where(height == 0, first_jump, 0.0)
+
+    def update():
+        def first(plane, carry):
+            share, jump = profile(plane)
+            QB[plane] = KX[plane] * (share * LP[0] + jump * LP[1])
+            return carry
+
+        lax.fori_loop(0, NZL + 2, first, 0)
+
+        def second(z, carry):
+            share, jump = profile(z + 1)
+            edges = KE[z] * (share * LE[0] + jump * LE[1])
+            wide = QB[z + 1]
+            bend = ring_sum(wide, edges, QB[z, inner], QB[z + 2, inner], KX[z + 1, inner])
+            raised, slope = share * LP[1, inner], wide[inner]
+            for c in range(NV):
+                S[0, c, z + 1] += twice[c] * raised + 2.0 * once[c] * slope + source[c] * bend
+            return carry
+
+        lax.fori_loop(0, NZL, second, 0)
+
     def sent_facts():
         @pl.when(on_wall)
         def _():
@@ -690,26 +726,11 @@
             part, part, rsend.at[it], rrecv.at[it], device_id=other_core, device_id_type=MESH
         )
 
-    around_wall = wall_copies(ITERS)
-
-    @pl.when(on_wall)
-    def _():
-        each(around_wall, lambda pair: pair[0].start())
-
     for it in range(ITERS - 1):
         n = 2 * it + 2
         pack(S.at[0])
         start_halo(n, S.at[0])
-        if it == 0:
-
-            @pl.when(on_wall)
-            def _():
-                each(around_wall, lambda pair: pair[1].wait_recv())
-                tell_faces()
-                each(around_wall, lambda pair: pair[0].wait_send())
-
-            send_facts()
-        else:
+        if it:
 
             @pl.when(is_solver)
             def _():
@@ -726,10 +747,11 @@
                 answer(it)
 
         finish_halo(n + 1, S.at[1])
-        sweep(n + 1, S.at[1], S.at[0])
+        sweep(n + 1, S.at[1], S.at[0], 0, 1)
         wall_base()
         sent_to_solvers(it)
         send_pressure(it + 1)
+        sweep(n + 1, S.at[1], S.at[0], 1, NZL)
         if it == 0:
 
             @pl.when(is_solver)
@@ -878,7 +900,9 @@
             pltpu.VMEM((NZL, CX, CY), F32),
             pltpu.VMEM((EBD, EB, EB), F32),
             pltpu.VMEM((EBD, EB, EB), F32),
-            pltpu.VMEM((EBD, 2 * EB, 2 * EB), BF16),
+            pltpu.VMEM((PAIRS, 2 * EB, 2 * EB), BF16),
+            pltpu.VMEM((PAIRS, 2 * EB, 2 * EB), BF16),
+            pltpu.VMEM((PAIRS, EB, 2 * EB), BF16),
             pltpu.VMEM((2, NV + 1, NZL, CY), F32),
             pltpu.VMEM((sweeps, 2, NV + 1, NZL, CY), F32),
             pltpu.VMEM((CX, CY), F32),

time: 87.6 us -> 88.1 us (level)
  no operation moved by 1% of the time
where the time goes in v7:
time: 88.1 us; the launch traced here: 88 us
  Pallas kernels  87.3 us (99%)
    pallas_call x1, Pallas kernels, on_device(): pl.pallas_call(kernel, out_shape=(jax.ShapeDtypeStruct(state.shape, F32),...  85.3 us
    pallas_call x1, Pallas kernels, on_device(): pl.pallas_call(last_add, out_shape=(jax.ShapeDtypeStruct(state.shape, F32...  2.06 us

profile of v7, /device:TPU:1, one launch (start us, length us, event | category | flops | bytes accessed | tf_op | source)
XLA Modules:
  0.0 88.0 jit_solution(4104021646747261065)
XLA Ops:
  0.6 85.3 %shard_map.122 = (f32[5,8,32,128]{3,2,1,0:T(8,128)}, f32[8,32,128]{2,1,0:T(8,128)}, f32[16,128]{1,0:T(8,128)}) custom-call(f32[5,8,32,128]{3,2,1,0:T(8,128)} %state_in.1, f32[8,32,128]{2,1,0:T(8,128)} %kappa_in.1, f32[5,5]{1,0:T(8,128)} %mix_in.1, f32[5]{0:T(128)} %press_in.1, f32[5]{0:T(128)} %source_in.3, f32[128,128]{1,0:T(8,128)} %interp_in.1, ...), custom_call_target="tpu_custom_call" | custom-call | tf_op jit(solution)/shard_map/pallas_call | solution.py:880
  85.9 2.1 %shard_map.123 = (f32[5,8,32,128]{3,2,1,0:T(8,128)}, f32[16,128]{1,0:T(8,128)}) custom-call(f32[5,8,32,128]{3,2,1,0:T(8,128)} %get-tuple-element.5.before, f32[8,32,128]{2,1,0:T(8,128)} %get-tuple-element.6.raised, f32[5]{0:T(128)} %source_in.3, f32[16,128]{1,0:T(8,128)} %get-tuple-element.7.displacement), custom_call_target="tpu_custom_call" | custom-call | tf_op jit(solution)/shard_map/pallas_call | solution.py:963

commit v8 on v7

--- a/solution.py
+++ b/solution.py
@@ -482,8 +482,40 @@
             CS[n + 1] = pick(selector, pltpu.roll(wall_coeff, (CXE - d) % CXE, 0)[inner])
         CS[4] = pick(selector, KX[2, inner])
 
+    half = FACES // 2
+    facts_core = ix // (NFX // 2)
+    facts_here = jnp.logical_and(is_solver, facts_core == iz)
+
     def send_facts():
-        send_to_solvers(lambda to: CS.at[:, pl.ds(CAP * to, CAP)], RC.at[:, own_rows], csend, crecv)
+        def send(to, home_y):
+            pltpu.make_async_remote_copy(
+                CS.at[:, pl.ds(CAP * to, CAP)], RC.at[:, own_rows], csend, crecv.at[0],
+                device_id=(to, home_y, facts_core), device_id_type=MESH,
+            ).start()
+
+        def group(step, carry):
+            for to, home_y in owners_at(step):
+                send(to, home_y)
+            return carry
+
+        @pl.when(on_wall)
+        def _():
+            lax.fori_loop(0, RING_Z - 1, group, 0)
+            for to, home_y in near_owners:
+                send(to, home_y)
+
+            @pl.when(facts_here)
+            def _():
+                pltpu.make_async_copy(CS.at[:, pl.ds(CAP * ix, CAP)], RC.at[:, own_rows], crecv.at[0]).start()
+
+            @pl.when(jnp.logical_not(facts_here))
+            def _():
+                send(ix, home)
+
+    share_facts = pltpu.make_async_remote_copy(
+        RC.at[:, pl.ds(half * iz, half)], RC.at[:, pl.ds(half * iz, half)], csend, crecv.at[1],
+        device_id=other_core, device_id_type=MESH,
+    )
 
     around_wall = wall_copies(ITERS)
     pack(S.at[0])
@@ -519,14 +551,6 @@
 
     lax.fori_loop(0, NZL, kappa_edges, 0)
 
-    @pl.when(on_wall)
-    def _():
-        each(around_wall, lambda pair: pair[1].wait_recv())
-        tell_faces()
-        each(around_wall, lambda pair: pair[0].wait_send())
-
-    send_facts()
-
     def wall_base():
         @pl.when(on_wall)
         def _():
@@ -541,6 +565,15 @@
     send_pressure(0)
     sweep(1, S.at[1], S.at[0], 1, NZL)
     sent_to_solvers(ITERS)
+
+    @pl.when(on_wall)
+    def _():
+        each(around_wall, lambda pair: pair[1].wait_recv())
+        tell_faces()
+        each(around_wall, lambda pair: pair[0].wait_send())
+
+    send_facts()
+
 
     @pl.when(is_solver)
     def _():
@@ -619,18 +652,23 @@
     def sent_facts():
         @pl.when(on_wall)
         def _():
-            @pl.when(is_solver)
-            def _():
-                rest = RC.at[:, pl.ds(0, CAP * (2 * NFX - 1))]
+            @pl.when(facts_here)
+            def _():
+                rest = RC.at[:, pl.ds(0, CAP * (NFX - 1))]
                 pltpu.make_async_copy(rest, rest, csend).wait()
 
-            @pl.when(not_solver)
-            def _():
-                rest = RC.at[:, pl.ds(0, CAP * 2 * NFX)]
+            @pl.when(jnp.logical_not(facts_here))
+            def _():
+                rest = RC.at[:, pl.ds(0, CAP * NFX)]
                 pltpu.make_async_copy(rest, rest, csend).wait()
 
+    def pass_facts():
+        mine = RC.at[:, pl.ds(half * iz, half)]
+        pltpu.make_async_copy(mine, mine, crecv.at[0]).wait()
+        share_facts.start()
+
     def hear_facts():
-        pltpu.make_async_copy(RC, RC, crecv).wait()
+        share_facts.wait()
         names = lax.broadcasted_iota(jnp.int32, (FACES, NFX * EBD), 1) + 1
         names = names.astype(F32)
         for m in range(AROUND):
@@ -741,10 +779,12 @@
         pack(S.at[1])
         start_halo(n + 1, S.at[1])
         if it == 0:
+            sent_facts()
 
             @pl.when(is_solver)
             def _():
                 answer(it)
+                pass_facts()
 
         finish_halo(n + 1, S.at[1])
         sweep(n + 1, S.at[1], S.at[0], 0, 1)
@@ -787,8 +827,6 @@
         def _():
             each(copies, lambda pair: pair[0].wait_send())
             beside_wall.wait_send()
-
-    sent_facts()
 
     last = ITERS - 1
     out = pltpu.make_async_copy(S.at[0, :, pl.ds(1, NZL)], state_out, load_sem.at[0])
@@ -949,7 +987,7 @@
             dma((ITERS,)),
             dma((ITERS,)),
             dma,
-            dma,
+            dma((2,)),
             dma((ITERS - 1,)),
             dma((ITERS - 1,)),
         ],

time: 88.1 us -> 86.2 us (0.978)
  Pallas kernels: 87.3 us -> 85.4 us
    pallas_call x1, Pallas kernels: 85.3 us -> 83.3 us  [on_device(): pl.pallas_call(kernel, out_shape=(jax.ShapeDtypeStruct(state.shape, F32),...]
where the time goes in v8:
time: 86.2 us; the launch traced here: 86 us
  Pallas kernels  85.4 us (99%)
    pallas_call x1, Pallas kernels, on_device(): pl.pallas_call(kernel, out_shape=(jax.ShapeDtypeStruct(state.shape, F32),...  83.3 us
    pallas_call x1, Pallas kernels, on_device(): pl.pallas_call(last_add, out_shape=(jax.ShapeDtypeStruct(state.shape, F32...  2.06 us

profile of v8, /device:TPU:1, one launch (start us, length us, event | category | flops | bytes accessed | tf_op | source)
XLA Modules:
  0.0 86.0 jit_solution(11061286761786070083)
XLA Ops:
  0.6 83.3 %shard_map.122 = (f32[5,8,32,128]{3,2,1,0:T(8,128)}, f32[8,32,128]{2,1,0:T(8,128)}, f32[16,128]{1,0:T(8,128)}) custom-call(f32[5,8,32,128]{3,2,1,0:T(8,128)} %state_in.1, f32[8,32,128]{2,1,0:T(8,128)} %kappa_in.1, f32[5,5]{1,0:T(8,128)} %mix_in.1, f32[5]{0:T(128)} %press_in.1, f32[5]{0:T(128)} %source_in.3, f32[128,128]{1,0:T(8,128)} %interp_in.1, ...), custom_call_target="tpu_custom_call" | custom-call | tf_op jit(solution)/shard_map/pallas_call | solution.py:918
  84.0 2.1 %shard_map.123 = (f32[5,8,32,128]{3,2,1,0:T(8,128)}, f32[16,128]{1,0:T(8,128)}) custom-call(f32[5,8,32,128]{3,2,1,0:T(8,128)} %get-tuple-element.5.before, f32[8,32,128]{2,1,0:T(8,128)} %get-tuple-element.6.raised, f32[5]{0:T(128)} %source_in.3, f32[16,128]{1,0:T(8,128)} %get-tuple-element.7.displacement), custom_call_target="tpu_custom_call" | custom-call | tf_op jit(solution)/shard_map/pallas_call | solution.py:1001

commit v9 on v8

--- a/solution.py
+++ b/solution.py
@@ -566,14 +566,6 @@
     sweep(1, S.at[1], S.at[0], 1, NZL)
     sent_to_solvers(ITERS)
 
-    @pl.when(on_wall)
-    def _():
-        each(around_wall, lambda pair: pair[1].wait_recv())
-        tell_faces()
-        each(around_wall, lambda pair: pair[0].wait_send())
-
-    send_facts()
-
 
     @pl.when(is_solver)
     def _():
@@ -768,7 +760,16 @@
         n = 2 * it + 2
         pack(S.at[0])
         start_halo(n, S.at[0])
-        if it:
+        if it == 0:
+
+            @pl.when(on_wall)
+            def _():
+                each(around_wall, lambda pair: pair[1].wait_recv())
+                tell_faces()
+                each(around_wall, lambda pair: pair[0].wait_send())
+
+            send_facts()
+        else:
 
             @pl.when(is_solver)
             def _():

time: 86.2 us -> 83.5 us (0.969)
  Pallas kernels: 85.4 us -> 82.7 us
    pallas_call x1, Pallas kernels: 83.3 us -> 80.7 us  [on_device(): pl.pallas_call(kernel, out_shape=(jax.ShapeDtypeStruct(state.shape, F32),...]
where the time goes in v9:
time: 83.5 us; the launch traced here: 83.4 us
  Pallas kernels  82.7 us (99%)
    pallas_call x1, Pallas kernels, on_device(): pl.pallas_call(kernel, out_shape=(jax.ShapeDtypeStruct(state.shape, F32),...  80.7 us
    pallas_call x1, Pallas kernels, on_device(): pl.pallas_call(last_add, out_shape=(jax.ShapeDtypeStruct(state.shape, F32...  2.06 us

profile of v9, /device:TPU:1, one launch (start us, length us, event | category | flops | bytes accessed | tf_op | source)
XLA Modules:
  0.0 83.4 jit_solution(13736152132572639914)
XLA Ops:
  0.6 80.7 %shard_map.122 = (f32[5,8,32,128]{3,2,1,0:T(8,128)}, f32[8,32,128]{2,1,0:T(8,128)}, f32[16,128]{1,0:T(8,128)}) custom-call(f32[5,8,32,128]{3,2,1,0:T(8,128)} %state_in.1, f32[8,32,128]{2,1,0:T(8,128)} %kappa_in.1, f32[5,5]{1,0:T(8,128)} %mix_in.1, f32[5]{0:T(128)} %press_in.1, f32[5]{0:T(128)} %source_in.3, f32[128,128]{1,0:T(8,128)} %interp_in.1, ...), custom_call_target="tpu_custom_call" | custom-call | tf_op jit(solution)/shard_map/pallas_call | solution.py:919
  81.3 2.1 %shard_map.123 = (f32[5,8,32,128]{3,2,1,0:T(8,128)}, f32[16,128]{1,0:T(8,128)}) custom-call(f32[5,8,32,128]{3,2,1,0:T(8,128)} %get-tuple-element.5.before, f32[8,32,128]{2,1,0:T(8,128)} %get-tuple-element.6.raised, f32[5]{0:T(128)} %source_in.3, f32[16,128]{1,0:T(8,128)} %get-tuple-element.7.displacement), custom_call_target="tpu_custom_call" | custom-call | tf_op jit(solution)/shard_map/pallas_call | solution.py:1002

commit v10 on v9

--- a/solution.py
+++ b/solution.py
@@ -756,6 +756,21 @@
             part, part, rsend.at[it], rrecv.at[it], device_id=other_core, device_id_type=MESH
         )
 
+    last = ITERS - 1
+
+    def disp_copy(t):
+        return pltpu.make_async_remote_copy(
+            DV, DR, osend.at[t], orecv.at[1], device_id=(ix, (iy + t) % NFY, iz), device_id_type=MESH
+        )
+
+    def answer_last():
+        answer(last)
+        back = lax.dot_general(placed, XV[...], (((0,), (0,)), ((), ())), precision=HIGHEST, preferred_element_type=F32)
+        DV[...] = back[:EBD]
+        for t in range(1, NFY):
+            disp_copy(t).start()
+        disp_out[...] = back[:EBD]
+
     for it in range(ITERS - 1):
         n = 2 * it + 2
         pack(S.at[0])
@@ -809,6 +824,8 @@
         @pl.when(is_solver)
         def _():
             respond(it)
+            if it == last - 1:
+                answer_last()
 
         beside_wall = relay(it, WN.at[it])
 
@@ -829,23 +846,8 @@
             each(copies, lambda pair: pair[0].wait_send())
             beside_wall.wait_send()
 
-    last = ITERS - 1
     out = pltpu.make_async_copy(S.at[0, :, pl.ds(1, NZL)], state_out, load_sem.at[0])
     out.start()
-
-    def disp_copy(t):
-        return pltpu.make_async_remote_copy(
-            DV, DR, osend.at[t], orecv.at[1], device_id=(ix, (iy + t) % NFY, iz), device_id_type=MESH
-        )
-
-    @pl.when(is_solver)
-    def _():
-        answer(last)
-        back = lax.dot_general(placed, XV[...], (((0,), (0,)), ((), ())), precision=HIGHEST, preferred_element_type=F32)
-        DV[...] = back[:EBD]
-        for t in range(1, NFY):
-            disp_copy(t).start()
-        disp_out[...] = back[:EBD]
 
     beside_wall = relay(last, WN.at[last, 1, pl.ds(PAD, CX)])
 

time: 83.5 us -> 81.4 us (0.975)
  Pallas kernels: 82.7 us -> 80.6 us
    pallas_call x1, Pallas kernels: 80.7 us -> 78.6 us  [on_device(): pl.pallas_call(kernel, out_shape=(jax.ShapeDtypeStruct(state.shape, F32),...]
where the time goes in v10:
time: 81.4 us; the launch traced here: 81.3 us
  Pallas kernels  80.6 us (99%)
    pallas_call x1, Pallas kernels, on_device(): pl.pallas_call(kernel, out_shape=(jax.ShapeDtypeStruct(state.shape, F32),...  78.6 us
    pallas_call x1, Pallas kernels, on_device(): pl.pallas_call(last_add, out_shape=(jax.ShapeDtypeStruct(state.shape, F32...  2.06 us

profile of v10, /device:TPU:1, one launch (start us, length us, event | category | flops | bytes accessed | tf_op | source)
XLA Modules:
  0.0 81.3 jit_solution(17703931994172404758)
XLA Ops:
  0.6 78.6 %shard_map.122 = (f32[5,8,32,128]{3,2,1,0:T(8,128)}, f32[8,32,128]{2,1,0:T(8,128)}, f32[16,128]{1,0:T(8,128)}) custom-call(f32[5,8,32,128]{3,2,1,0:T(8,128)} %state_in.1, f32[8,32,128]{2,1,0:T(8,128)} %kappa_in.1, f32[5,5]{1,0:T(8,128)} %mix_in.1, f32[5]{0:T(128)} %press_in.1, f32[5]{0:T(128)} %source_in.3, f32[128,128]{1,0:T(8,128)} %interp_in.1, ...), custom_call_target="tpu_custom_call" | custom-call | tf_op jit(solution)/shard_map/pallas_call | solution.py:921
  79.2 2.1 %shard_map.123 = (f32[5,8,32,128]{3,2,1,0:T(8,128)}, f32[16,128]{1,0:T(8,128)}) custom-call(f32[5,8,32,128]{3,2,1,0:T(8,128)} %get-tuple-element.5.before, f32[8,32,128]{2,1,0:T(8,128)} %get-tuple-element.6.raised, f32[5]{0:T(128)} %source_in.3, f32[16,128]{1,0:T(8,128)} %get-tuple-element.7.displacement), custom_call_target="tpu_custom_call" | custom-call | tf_op jit(solution)/shard_map/pallas_call | solution.py:1004

commit v11 on v10

--- a/solution.py
+++ b/solution.py
@@ -406,30 +406,33 @@
     for load in loads[5:]:
         load.wait()
 
-    @pl.when(is_solver)
-    def _():
-        def parts(k):
-            block = order[0, k]
-            inverse = BI[block]
-            force_part = lax.dot_general(interp[...], inverse, NT, precision=HIGHEST, preferred_element_type=F32)
-            chain = jnp.dot(inverse, CO[block], precision=HIGHEST, preferred_element_type=F32)
-            return force_part, -chain.T
-
-        def both_parts(matrix):
-            high, low = split(matrix)
-            return jnp.concatenate([high, low], axis=1)
-
-        def products(m, carry):
-            force, chain = parts(2 * m)
-            next_force, next_chain = parts(2 * m + 1)
-            passed = jnp.dot(force, next_chain, precision=HIGHEST, preferred_element_type=F32)
-            leap = jnp.dot(chain, next_chain, precision=HIGHEST, preferred_element_type=F32)
-            R[m] = both_parts(jnp.concatenate([force, chain], axis=0))
-            RO[m] = both_parts(jnp.concatenate([next_force, passed], axis=0))
-            RN[m] = both_parts(leap)
-            return carry
-
-        lax.fori_loop(0, PAIRS, products, 0)
+    def parts(k):
+        block = order[0, k]
+        inverse = BI[block]
+        force_part = lax.dot_general(interp[...], inverse, NT, precision=HIGHEST, preferred_element_type=F32)
+        chain = jnp.dot(inverse, CO[block], precision=HIGHEST, preferred_element_type=F32)
+        return force_part, -chain.T
+
+    def both_parts(matrix):
+        high, low = split(matrix)
+        return jnp.concatenate([high, low], axis=1)
+
+    def products(m, carry):
+        force, chain = parts(2 * m)
+        next_force, next_chain = parts(2 * m + 1)
+        passed = jnp.dot(force, next_chain, precision=HIGHEST, preferred_element_type=F32)
+        leap = jnp.dot(chain, next_chain, precision=HIGHEST, preferred_element_type=F32)
+        R[m] = both_parts(jnp.concatenate([force, chain], axis=0))
+        RO[m] = both_parts(jnp.concatenate([next_force, passed], axis=0))
+        RN[m] = both_parts(leap)
+        return carry
+
+    def multiply(first, end):
+        @pl.when(is_solver)
+        def _():
+            lax.fori_loop(first, end, products, 0)
+
+    multiply(0, PAIRS // 2)
 
     numbers = range(NV)
     source = [source_weight[c] for c in numbers]
@@ -528,6 +531,7 @@
 
     kappa_plane.start()
     send_rows(ITERS, SL)
+    multiply(PAIRS // 2, PAIRS)
     finish_halo(0, S.at[0])
     sweep(0, S.at[0], S.at[1])
     pack(S.at[1])

time: 81.4 us -> 80 us (0.983)
  Pallas kernels: 80.6 us -> 79.2 us
    pallas_call x1, Pallas kernels: 78.6 us -> 77.2 us  [on_device(): pl.pallas_call(kernel, out_shape=(jax.ShapeDtypeStruct(state.shape, F32),...]
where the time goes in v11:
time: 80 us; the launch traced here: 79.9 us
  Pallas kernels  79.2 us (99%)
    pallas_call x1, Pallas kernels, on_device(): pl.pallas_call(kernel, out_shape=(jax.ShapeDtypeStruct(state.shape, F32),...  77.2 us
    pallas_call x1, Pallas kernels, on_device(): pl.pallas_call(last_add, out_shape=(jax.ShapeDtypeStruct(state.shape, F32...  2.06 us

profile of v11, /device:TPU:1, one launch (start us, length us, event | category | flops | bytes accessed | tf_op | source)
XLA Modules:
  0.0 79.9 jit_solution(16972728097732825858)
XLA Ops:
  0.6 77.2 %shard_map.122 = (f32[5,8,32,128]{3,2,1,0:T(8,128)}, f32[8,32,128]{2,1,0:T(8,128)}, f32[16,128]{1,0:T(8,128)}) custom-call(f32[5,8,32,128]{3,2,1,0:T(8,128)} %state_in.1, f32[8,32,128]{2,1,0:T(8,128)} %kappa_in.1, f32[5,5]{1,0:T(8,128)} %mix_in.1, f32[5]{0:T(128)} %press_in.1, f32[5]{0:T(128)} %source_in.3, f32[128,128]{1,0:T(8,128)} %interp_in.1, ...), custom_call_target="tpu_custom_call" | custom-call | tf_op jit(solution)/shard_map/pallas_call | solution.py:925
  77.8 2.1 %shard_map.123 = (f32[5,8,32,128]{3,2,1,0:T(8,128)}, f32[16,128]{1,0:T(8,128)}) custom-call(f32[5,8,32,128]{3,2,1,0:T(8,128)} %get-tuple-element.5.before, f32[8,32,128]{2,1,0:T(8,128)} %get-tuple-element.6.raised, f32[5]{0:T(128)} %source_in.3, f32[16,128]{1,0:T(8,128)} %get-tuple-element.7.displacement), custom_call_target="tpu_custom_call" | custom-call | tf_op jit(solution)/shard_map/pallas_call | solution.py:1008
